TPU v7x, 32 devices: a whole 2x2x4 slice. The times are simulated.
32 devices in a mesh: row: 8 (over z, x), col: 4 (over y, core).
Axes of the slice: x: 2, y: 2, z: 4, core: 2. Of those that a mesh axis runs over, the one named last changes fastest.
Arguments:
- homolog_matrix: bfloat16 [64, 320, 64], P('row', 'col'), may hold values from -6 to 6
- contact_matrix: bfloat16 [320, 320, 128], P('row', 'col'), may hold values from -24 to 24
- genuine_homolog_total: int32 [1], replicated, may hold values from 1 to 64
- genuine_chain_length: int32 [1], replicated, may hold values from 160 to 320
- tensor_product_matrices: bfloat16 [1, 64, 64], replicated, may hold values from -0.75 to 0.75
- tensor_product_final: bfloat16 [1, 1024, 128], replicated, may hold values from -0.75 to 0.75
- mixing_value_gate_matrix: bfloat16 [1, 64, 512], replicated, may hold values from -0.75 to 0.75
- mixing_logit_matrix: bfloat16 [1, 128, 8], replicated
- mixing_final_matrix: bfloat16 [1, 256, 64], replicated, may hold values from -1.5 to 1.5
- feedforward_gate_expand: bfloat16 [1, 128, 1024], replicated, may hold values from -0.5 to 0.5
- feedforward_shrink_matrix: bfloat16 [1, 512, 128], replicated, may hold values from -0.25 to 0.25
Outputs:
- msa_out: bfloat16 [64, 320, 64], P('row', 'col')
- pair_out: bfloat16 [320, 320, 128], P('row', 'col')
Inputs may be any that keep to these rules, and one draw needn't show every extreme that they name: Sequences from genuine_homolog_total on are padding. Residues from genuine_chain_length on are padding.
All inputs are finite; a program needn't handle non-finite values.
Results may differ from a plain program's by a relative error of at most 0.0065.
The roundings to bfloat16 on the way count: a program that leaves them out, or rounds other values in their place, can miss the bound.
Values may be sent and summed in bfloat16 or wider, within the bound.
A program may use at most 64 MiB of HBM per device.

v0:
```python
import jax
import jax.numpy as jnp
from jax import lax
from jax.sharding import PartitionSpec as P

EPSILON = 1e-05
MASKED = -1000000000.0


def broadcast(value, axis, source):
    kept = jnp.where(lax.axis_index(axis) == source, value, 0).astype(value.dtype)
    return lax.psum(kept, axis)


def standardize_features(field):
    field = field.astype(jnp.float32)
    center = field - jnp.mean(field, axis=-1, keepdims=True)
    spread = jnp.mean(center * center, axis=-1, keepdims=True)
    return center * lax.rsqrt(spread + EPSILON)


def local(
    homolog_matrix,
    contact_matrix,
    genuine_homolog_total,
    genuine_chain_length,
    tensor_product_matrices,
    tensor_product_final,
    mixing_value_gate_matrix,
    mixing_logit_matrix,
    mixing_final_matrix,
    feedforward_gate_expand,
    feedforward_shrink_matrix,
):
    homolog_rows_local, chain_positions_local, homolog_rows_full = homolog_matrix.shape
    rows_dev = contact_matrix.shape[0]
    pair_width = contact_matrix.shape[2]
    outer_width = tensor_product_matrices.shape[2] // 2
    head_count = mixing_logit_matrix.shape[2]
    hidden_width = mixing_final_matrix.shape[1]
    head_width = hidden_width // head_count
    trans_width = feedforward_shrink_matrix.shape[1]
    row_blocks = rows_dev // 8
    row_index = lax.axis_index("row")
    col_index = lax.axis_index("col")
    ratio = lax.axis_size("row") // lax.axis_size("col")
    total_seqs = homolog_rows_local * lax.axis_size("row")
    seq_ids = row_index * homolog_rows_local + jnp.arange(homolog_rows_local, dtype=jnp.int32)
    res_ids = col_index * chain_positions_local + jnp.arange(chain_positions_local, dtype=jnp.int32)
    pair_ids = row_index * rows_dev + jnp.arange(rows_dev, dtype=jnp.int32)
    seq_float = (seq_ids < genuine_homolog_total[0]).astype(jnp.float32)
    res_valid = res_ids < genuine_chain_length[0]
    res_float = res_valid.astype(jnp.float32)
    row_float = (pair_ids < genuine_chain_length[0]).astype(jnp.float32)
    divisor = jnp.maximum(
        genuine_homolog_total[0].astype(jnp.float32) * row_float[:, None] * res_float[None, :], 1.0
    )
    starts = jnp.arange(row_blocks, dtype=jnp.int32) * 8
    standardized_source = standardize_features(homolog_matrix).astype(jnp.bfloat16)
    reshaped_tensor = standardized_source.reshape(
        homolog_rows_local * chain_positions_local, homolog_rows_full
    )
    projected = jnp.dot(
        reshaped_tensor, tensor_product_matrices[0], preferred_element_type=jnp.float32
    ).reshape(homolog_rows_local, chain_positions_local, 2 * outer_width)
    projected = (projected * (seq_float[:, None, None] * res_float[None, :, None])).astype(
        jnp.bfloat16
    )
    packed = projected.reshape(homolog_rows_local, chain_positions_local * 2 * outer_width)
    columns = lax.all_gather(packed, "row", axis=0, tiled=True).reshape(
        total_seqs, chain_positions_local, 2 * outer_width
    )
    left_all = columns[:, :, :outer_width].reshape(total_seqs, chain_positions_local * outer_width)
    right = columns[:, :, outer_width:].reshape(total_seqs, chain_positions_local * outer_width)
    left_cols = broadcast(left_all, "col", row_index // ratio).reshape(
        total_seqs, chain_positions_local, outer_width
    )
    left = lax.dynamic_slice_in_dim(left_cols, row_index % ratio * rows_dev, rows_dev, 1)
    outer_weight = tensor_product_final[0]

    def outer_rows(inputs):
        start, pair_rows = inputs
        rows = lax.dynamic_slice_in_dim(left, start, 8, 1).reshape(total_seqs, 8 * outer_width)
        product = lax.dot_general(
            rows, right, (((0,), (0,)), ((), ())), preferred_element_type=jnp.float32
        )
        product = product.reshape(8, outer_width, chain_positions_local, outer_width).transpose(
            0, 2, 1, 3
        )
        product = product.reshape(8, chain_positions_local, outer_width * outer_width)
        scale = lax.dynamic_slice_in_dim(divisor, start, 8, 0)
        outer = (product / scale[:, :, None]).astype(jnp.bfloat16)
        update = jnp.dot(
            outer.reshape(8 * chain_positions_local, outer_width * outer_width),
            outer_weight,
            preferred_element_type=jnp.float32,
        )
        return (
            pair_rows.astype(jnp.float32) + update.reshape(8, chain_positions_local, pair_width)
        ).astype(jnp.bfloat16)

    contact_matrix = lax.map(
        outer_rows,
        (starts, contact_matrix.reshape(row_blocks, 8, chain_positions_local, pair_width)),
    ).reshape(rows_dev, chain_positions_local, pair_width)
    bias_weight = mixing_logit_matrix[0]

    def norm_rows(pair_rows):
        normed_rows = standardize_features(pair_rows).astype(jnp.bfloat16)
        logit_rows = jnp.dot(
            normed_rows.reshape(8 * chain_positions_local, pair_width),
            bias_weight,
            preferred_element_type=jnp.float32,
        )
        return (normed_rows, logit_rows.reshape(8, chain_positions_local, head_count))

    pair_normed, logits = lax.map(
        norm_rows, contact_matrix.reshape(row_blocks, 8, chain_positions_local, pair_width)
    )
    logits = jnp.where(
        res_valid[None, :, None],
        logits.reshape(rows_dev, chain_positions_local, head_count),
        MASKED,
    )
    logits = logits.transpose(0, 2, 1)
    peak = lax.pmax(jnp.max(logits, axis=2), "col")
    expo = jnp.exp(logits - peak[:, :, None])
    totals = lax.psum(jnp.sum(expo, axis=2), "col")
    local_weights = (expo / totals[:, :, None]).astype(jnp.bfloat16)
    part_rows = rows_dev // lax.axis_size("row")
    sectioned = local_weights.reshape(1, rows_dev, head_count, 1, chain_positions_local)
    moved = lax.all_to_all(
        lax.all_to_all(sectioned, "row", split_axis=1, concat_axis=0, tiled=True),
        "col",
        split_axis=0,
        concat_axis=3,
        tiled=True,
    )
    moved = moved.reshape(
        ratio, part_rows, head_count, lax.axis_size("col") * chain_positions_local
    )
    mine = lax.all_gather(moved, "row", axis=1, tiled=True).reshape(
        chain_positions_local, head_count, lax.axis_size("col") * chain_positions_local
    )
    value_weight = mixing_value_gate_matrix[0][:, :hidden_width]
    gate_weight = mixing_value_gate_matrix[0][:, hidden_width:]
    gate = jax.nn.sigmoid(
        jnp.dot(reshaped_tensor, gate_weight, preferred_element_type=jnp.float32)
    ).reshape(homolog_rows_local, chain_positions_local, hidden_width)
    values_local = jnp.dot(reshaped_tensor, value_weight, preferred_element_type=jnp.float32)
    values_local = values_local.astype(jnp.bfloat16).reshape(
        homolog_rows_local, chain_positions_local, hidden_width
    )
    values_piece = lax.all_gather(values_local, "col", axis=1, tiled=True)
    count = values_piece.shape[1]
    heads_piece = values_piece.reshape(homolog_rows_local, count, head_count, head_width)
    averaged = jnp.einsum("ihj,sjhc->sihc", mine, heads_piece, preferred_element_type=jnp.float32)
    gated = (
        gate * averaged.reshape(homolog_rows_local, chain_positions_local, hidden_width)
    ).astype(jnp.bfloat16)
    contact_increment = jnp.dot(
        gated.reshape(homolog_rows_local * chain_positions_local, hidden_width),
        mixing_final_matrix[0],
        preferred_element_type=jnp.float32,
    )
    homolog_matrix = (
        homolog_matrix.astype(jnp.float32)
        + contact_increment.reshape(homolog_rows_local, chain_positions_local, homolog_rows_full)
    ).astype(jnp.bfloat16)
    up_weight = feedforward_gate_expand[0]
    down_weight = feedforward_shrink_matrix[0]

    def transition_rows(inputs):
        pair_rows, normed_rows = inputs
        hidden = jnp.dot(
            normed_rows.reshape(8 * chain_positions_local, pair_width),
            up_weight,
            preferred_element_type=jnp.float32,
        )
        active = (jax.nn.silu(hidden[:, :trans_width]) * hidden[:, trans_width:]).astype(
            jnp.bfloat16
        )
        update = jnp.dot(active, down_weight, preferred_element_type=jnp.float32)
        return (
            pair_rows.astype(jnp.float32) + update.reshape(8, chain_positions_local, pair_width)
        ).astype(jnp.bfloat16)

    contact_matrix = lax.map(
        transition_rows,
        (contact_matrix.reshape(row_blocks, 8, chain_positions_local, pair_width), pair_normed),
    )
    contact_matrix = contact_matrix.reshape(rows_dev, chain_positions_local, pair_width)
    return (homolog_matrix, contact_matrix)


def solution(mesh):
    in_specs = (
        P("row", "col", None),
        P("row", "col", None),
        P(),
        P(),
        P(),
        P(),
        P(),
        P(),
        P(),
        P(),
        P(),
    )
    out_specs = (P("row", "col", None), P("row", "col", None))
    return jax.shard_map(local, mesh=mesh, in_specs=in_specs, out_specs=out_specs, check_vma=False)
```

profile of v0, /device:TPU:0, one launch (start us, length us, event | category | flops | bytes accessed | tf_op | source)
XLA Modules:
  0.0 227.5 jit_solution(14530378645405625014)
XLA Ops:
  8.5 0.9 convert_reduce_fusion.1
  9.5 1.0 fusion.39
  10.5 0.9 fusion.40
  11.5 0.9 fusion.35
  12.8 33.5 %all_gather.10 = bf16[64,5120]{1,0:T(8,128)(2,1)S(1)} all-gather(bf16[8,5120]{1,0:T(8,128)(2,1)S(1)} %reshape.211), channel_id=1, replica_groups=mesh['row'=8,'col'=4] {'row'}, dimensions={0}, use_global_device_ids=true | all-gather | bytes 737280 | tf_op jit(solution)/shard_map/all_gather | solution.py:70
  46.3 0.8 reshape.212
  47.1 1.5 fusion.49
  48.8 0.8 copy.53
  49.8 39.0 %all-reduce.2.cloned.1.call-done = bf16[64,80,32]{2,1,0:T(8,128)(2,1)} async-done(((bf16[64,80,32]{2,1,0:T(8,128)(2,1)}), bf16[64,80,32]{2,1,0:T(8,128)(2,1)}) %all-reduce.2.cloned.1.call-update) | async-done | bytes 327696 | tf_op jit(solution)/shard_map/psum | solution.py:12
  88.9 1.2 constant_dynamic-slice_fusion.2
  90.6 43.2 %while.32 = (s32[]{:T(128)}, bf16[5,8,80,128]{3,2,1,0:T(8,128)(2,1)S(1)}, bf16[5,8,80,128]{3,2,1,0:T(8,128)(2,1)}, s32[5]{0:T(128)S(1)}, bf16[64,40,32]{0,2,1:T(...) while((s32[]{:T(128)}, ...), condition=%wide.region_4.5_spmd, body=%wide.region_3.4_spmd.sunk | while | flops 253214720 | bytes 15736487 | solution.py:102
  90.6 0.7 dynamic_slice.57
  93.3 0.7 copy.72
  94.0 0.7 convolution_bitcast_fusion.3
  94.7 2.4 %copy.73 = f32[8,80,32,32]{1,3,2,0:T(8,128)S(1)} copy(f32[8,80,32,32]{1,2,3,0:T(8,128)S(1)} %convolution_bitcast_fusion.3) | data formatting | bytes 5242880 | tf_op jit(solution)/shard_map/while/body/eval_jaxpr/transpose | solution.py:87
  97.5 1.7 fusion.83
  99.2 0.7 dynamic_slice.57
  101.9 0.7 copy.72
  102.7 0.7 convolution_bitcast_fusion.3
  103.4 2.4 %copy.73 = f32[8,80,32,32]{1,3,2,0:T(8,128)S(1)} copy(f32[8,80,32,32]{1,2,3,0:T(8,128)S(1)} %convolution_bitcast_fusion.3) | data formatting | bytes 5242880 | tf_op jit(solution)/shard_map/while/body/eval_jaxpr/transpose | solution.py:87
  106.1 1.7 fusion.83
  107.8 0.7 dynamic_slice.57
  110.6 0.7 copy.72
  111.3 0.7 convolution_bitcast_fusion.3
  112.0 2.4 %copy.73 = f32[8,80,32,32]{1,3,2,0:T(8,128)S(1)} copy(f32[8,80,32,32]{1,2,3,0:T(8,128)S(1)} %convolution_bitcast_fusion.3) | data formatting | bytes 5242880 | tf_op jit(solution)/shard_map/while/body/eval_jaxpr/transpose | solution.py:87
  114.8 1.7 fusion.83
  116.5 0.7 dynamic_slice.57
  119.2 0.7 copy.72
  119.9 0.7 convolution_bitcast_fusion.3
  120.6 2.4 %copy.73 = f32[8,80,32,32]{1,3,2,0:T(8,128)S(1)} copy(f32[8,80,32,32]{1,2,3,0:T(8,128)S(1)} %convolution_bitcast_fusion.3) | data formatting | bytes 5242880 | tf_op jit(solution)/shard_map/while/body/eval_jaxpr/transpose | solution.py:87
  123.4 1.7 fusion.83
  125.1 0.7 dynamic_slice.57
  127.8 0.7 copy.72
  128.6 0.7 convolution_bitcast_fusion.3
  129.3 2.4 %copy.73 = f32[8,80,32,32]{1,3,2,0:T(8,128)S(1)} copy(f32[8,80,32,32]{1,2,3,0:T(8,128)S(1)} %convolution_bitcast_fusion.3) | data formatting | bytes 5242880 | tf_op jit(solution)/shard_map/while/body/eval_jaxpr/transpose | solution.py:87
  132.0 1.7 fusion.83
  133.9 5.9 %while.33 = (s32[]{:T(128)}, bf16[5,8,80,128]{3,2,1,0:T(8,128)(2,1)S(1)}, f32[5,8,80,8]{2,3,1,0:T(8,128)S(1)}, bf16[5,8,80,128]{3,2,1,0:T(8,128)(2,1)S(1)}, bf16[128,8]{0,1:T(8,128)(2,1)S(1)}, /*index=5*/s32[]{:T(128)}) while((s32[]{:T(128)}, bf16[5,8,80,128]{3,2,1,0:T(8,128)(2,1)S(1)}, f32[5,8,80,8]{2,3,1,0:T(8,128)S(1)}, ...), condition=%wide.region_8.9_spmd, body=%wide.region_5.8_spmd.sunk | while | flops 2458242 | bytes 889425 | solution.py:117
  139.9 10.4 %pmax.7 = f32[40,8]{1,0:T(8,128)S(1)} all-reduce(f32[40,8]{1,0:T(8,128)S(1)} %bitcast_reduce_fusion), channel_id=1, replica_groups=mesh['row'=8,'col'=4] {'col'}, use_global_device_ids=true, to_apply=%region_10.11 | all-reduce | flops 320 | bytes 2560 | tf_op jit(solution)/shard_map/pmax | solution.py:126
  150.5 10.3 %psum.15 = f32[40,8]{1,0:T(8,128)S(1)} all-reduce(f32[40,8]{1,0:T(8,128)S(1)} %fusion.42), channel_id=1, replica_groups=mesh['row'=8,'col'=4] {'col'}, use_global_device_ids=true, to_apply=%region_12.13 | all-reduce | flops 320 | bytes 2560 | tf_op jit(solution)/shard_map/psum | solution.py:128
  160.7 0.8 fusion.43
  161.5 5.6 %all-to-all-start = ((bf16[1,40,8,1,80]{4,2,3,0,1:T(8,128)(2,1)}), bf16[1,40,8,1,80]{4,2,3,0,1:T(8,128)(2,1)}, u32[]{:S(2)}, u32[]{:S(2)}) async-start(bf16[1,40,8,1,80]{4,2,3,0,1:T(8,128)(2,1)} %fusion.43), calls=%async_computation | async-start | bytes 163840 | tf_op jit(solution)/shard_map/all_to_all | solution.py:133
  167.5 0.8 copy.49
  168.4 5.9 %all-to-all-done = bf16[1,40,8,1,80]{4,2,3,0,1:T(8,128)(2,1)} async-done(((bf16[1,40,8,1,80]{4,2,3,0,1:T(8,128)(2,1)}), bf16[1,40,8,1,80]{4,2,3,0,1:T(8,128)(2,1)}, u32[]{:S(2)}, u32[]{:S(2)}) %all-to-all-start) | async-done | bytes 51232 | tf_op jit(solution)/shard_map/all_to_all | solution.py:133
  174.3 3.5 %all-to-all-start.1 = ((bf16[8,5,8,1,80]{4,2,1,3,0:T(8,128)(2,1)}), bf16[8,5,8,1,80]{4,2,1,3,0:T(8,128)(2,1)S(1)}, u32[]{:S(2)}, u32[]{:S(2)}) async-start(bf16[8,5,8,1,80]{4,2,1,3,0:T(8,128)(2,1)} %bitcast.35), calls=%async_computation.1 | async-start | bytes 163840 | tf_op jit(solution)/shard_map/all_to_all | solution.py:132
  177.9 5.4 %while.34 = (s32[]{:T(128)}, bf16[5,8,80,128]{3,2,1,0:T(8,128)(2,1)S(1)}, bf16[5,8,80,128]{3,2,1,0:T(8,128)(2,1)S(1)}, bf16[5,8,80,128]{3,2,1,0:T(8,128)(2,1)S(1...) while((s32[]{:T(128)}, bf16[5,8,80,128]{3,2,1,0:T(8,128)(2,1)S(1)}, ...), condition=%wide.region_14.15_spmd, body=%wide.region_13.14_spmd.sunk | while | flops 253870080 | bytes 7110741 | solution.py:188
  183.5 31.5 %all_gather.11 = bf16[2,40,8,320]{3,2,1,0:T(8,128)(2,1)S(1)} all-gather(bf16[2,5,8,320]{3,2,1,0:T(8,128)(2,1)S(1)} %reshape.217), channel_id=1, replica_groups=mesh['row'=8,'col'=4] {'row'}, dimensions={1}, use_global_device_ids=true | all-gather | bytes 460800 | tf_op jit(solution)/shard_map/all_gather | solution.py:142
  215.1 2.0 copy.50
  219.7 0.9 fusion.36
  (110 shorter events, 17.8 us)
Async XLA Ops:
  7.2 212.0 %copy-start = (bf16[1,256,64]{1,2,0:T(8,128)(2,1)S(1)}, bf16[1,256,64]{1,2,0:T(8,128)(2,1)}, u32[]{:S(2)}) copy-start(bf16[1,256,64]{1,2,0:T(8,128)(2,1)} %param.25) | copy-start | bytes 98308
  7.2 81.7 %all-reduce.2.cloned.1.call-start = ((), (), s32[]{:S(2)}) async-start(), calls=%async_computation.3 | async-start | bytes 2621440 | tf_op jit(solution)/shard_map/psum | solution.py:12
  49.8 40.7 %copy-start.1 = (bf16[1,1024,128]{2,1,0:T(8,128)(2,1)S(1)}, bf16[1,1024,128]{2,1,0:T(8,128)(2,1)}, u32[]{:S(2)}) copy-start(bf16[1,1024,128]{2,1,0:T(8,128)(2,1)} %param.22) | copy-start | bytes 786436
  90.5 43.3 %copy-start.7 = (bf16[1,128,8]{1,2,0:T(8,128)(2,1)S(1)}, bf16[1,128,8]{1,2,0:T(8,128)(2,1)}, u32[]{:S(2)}) copy-start(bf16[1,128,8]{1,2,0:T(8,128)(2,1)} %param.24) | copy-start | bytes 6148
  133.9 33.4 %copy-start.5 = (bf16[1,64,512]{2,1,0:T(8,128)(2,1)S(1)}, bf16[1,64,512]{2,1,0:T(8,128)(2,1)}, u32[]{:S(2)}) copy-start(bf16[1,64,512]{2,1,0:T(8,128)(2,1)} %param.23) | copy-start | bytes 196612
  139.9 38.0 %copy-start.2 = (bf16[1,128,1024]{2,1,0:T(8,128)(2,1)S(1)}, bf16[1,128,1024]{2,1,0:T(8,128)(2,1)}, u32[]{:S(2)}) copy-start(bf16[1,128,1024]{2,1,0:T(8,128)(2,1)} %param.26) | copy-start | bytes 786436
  139.9 38.0 %copy-start.6 = (bf16[1,512,128]{2,1,0:T(8,128)(2,1)S(1)}, bf16[1,512,128]{2,1,0:T(8,128)(2,1)}, u32[]{:S(2)}) copy-start(bf16[1,512,128]{2,1,0:T(8,128)(2,1)} %param.27) | copy-start | bytes 393220
  161.5 12.7 %all-to-all-start = ((bf16[1,40,8,1,80]{4,2,3,0,1:T(8,128)(2,1)}), bf16[1,40,8,1,80]{4,2,3,0,1:T(8,128)(2,1)}, u32[]{:S(2)}, u32[]{:S(2)}) async-start(bf16[1,40,8,1,80]{4,2,3,0,1:T(8,128)(2,1)} %fusion.43), calls=%async_computation | async-start | bytes 163840 | tf_op jit(solution)/shard_map/all_to_all | solution.py:133
  167.2 47.9 %all-gather.2.cloned.1.call-start = ((), (), s32[]{:S(2)}) async-start(), calls=%async_computation.2 | async-start | bytes 1638400 | tf_op jit(solution)/shard_map/all_gather | solution.py:154
  174.3 9.1 %all-to-all-start.1 = ((bf16[8,5,8,1,80]{4,2,1,3,0:T(8,128)(2,1)}), bf16[8,5,8,1,80]{4,2,1,3,0:T(8,128)(2,1)S(1)}, u32[]{:S(2)}, u32[]{:S(2)}) async-start(bf16[8,5,8,1,80]{4,2,1,3,0:T(8,128)(2,1)} %bitcast.35), calls=%async_computation.1 | async-start | bytes 163840 | tf_op jit(solution)/shard_map/all_to_all | solution.py:132
  183.3 33.7 %copy-start.4 = (bf16[5,8,80,128]{3,2,1,0:T(8,128)(2,1)}, bf16[5,8,80,128]{3,2,1,0:T(8,128)(2,1)S(1)}, u32[]{:S(2)}) copy-start(bf16[5,8,80,128]{3,2,1,0:T(8,128)(2,1)S(1)} %get-tuple-element.107) | copy-start | bytes 2457604
  218.8 0.9 copy-start.3
Sparse Core Ops, SparseCore 0:
  48.8 40.0 all-reduce.1
  169.5 19.9 all-gather.1
where the time goes:
time: 228 us; the launch traced here: 227 us
  blocking collectives  85.6 us (38%)
  waiting for transfers between devices  45 us (20%)
  local copies, waits for them, and re-layouts  27.9 us (12%)
  matrix products  21.6 us (9%)
  between operations  15.7 us (7%)
  other arithmetic  11.6 us (5%)
  loops' own time  10.9 us (5%)
  starting transfers between devices  9.17 us (4%)
    psum x1, waiting for transfers between devices, broadcast(): return lax.psum(kept, axis)  39 us
    all_gather x1, blocking collectives, local(): lax.all_gather(packed, 'row', axis=0, tiled=True)  33.5 us
    all_gather x1, blocking collectives, local(): lax.all_gather(moved, 'row', axis=1, tiled=True)  31.5 us
    transpose x5, local copies, waits for them, and re-layouts, outer_rows(): product.reshape(8, outer_width, chain_positions_local, outer_width)  11.9 us
    another operation x1, loops' own time, local(): lax.map(outer_rows, (starts, contact_matrix.reshape(row_blocks, 8, chain_...  10.6 us
    pmax x1, blocking collectives, local(): peak = lax.pmax(jnp.max(logits, axis=2), 'col')  10.4 us
    psum x1, blocking collectives, local(): totals = lax.psum(jnp.sum(expo, axis=2), 'col')  10.3 us
    dot_general x5, matrix products, outer_rows(): jnp.dot(outer.reshape(8 * chain_positions_local, outer_width * outer_widt...  8.51 us
  transfers between devices with their start and end apart: 4, of which 2 were waited for; matrix products, arithmetic and copies ran while one was open for 3% of the time, Pallas kernels for 0%

commit v1 on v0

v1 whole, which is shorter than its diff:
```python
import functools

import jax
import jax.numpy as jnp
from jax import lax
from jax.experimental import pallas as pl
from jax.experimental.pallas import tpu as pltpu
from jax.sharding import PartitionSpec as P

EPSILON = 1e-05
MASKED = -1000000000.0
MESH = pl.DeviceIdType.MESH
LANES = 128
BF16 = jnp.bfloat16
F32 = jnp.float32


def standardize_features(field):
    field = field.astype(F32)
    center = field - jnp.mean(field, axis=-1, keepdims=True)
    spread = jnp.mean(center * center, axis=-1, keepdims=True)
    return center * lax.rsqrt(spread + EPSILON)


def kernel(
    dims,
    seqs_ref, length_ref,
    right_ref, left_ref, normed_ref, homolog_ref, pair_ref,
    outer_w_ref, value_w_ref, gate_w_ref, logit_w_ref, final_w_ref, up_ref, down_ref,
    msa_ref, out_ref,
    right_buf, left_buf, normed_buf, logit_send, logit_buf,
    right_all, left_all, product, pair_new, pair_normed, values, gates, gated,
    s_right, r_right, s_left, r_left, s_norm, r_norm, s_logit, r_logit,
):
    R, C, ratio, rows, cols, width, heads, chunks = dims
    r = lax.axis_index("row")
    c = lax.axis_index("col")
    home = r // ratio

    barrier = pltpu.get_barrier_semaphore()

    def greet(row, col):
        pl.semaphore_signal(barrier, inc=1, device_id=(row, col), device_id_type=MESH)

    for t in range(1, R):
        greet((r + t) % R, c)
    for t in range(1, C):
        greet(r, (c + t) % C)
    for t in range(R):
        row = (r + t) % R

        @pl.when(jnp.logical_not((row == r) & (home == c)))
        def _():
            greet(row, home)

    for h in range(ratio):
        for t in range(C):
            row, col = c * ratio + h, (c + t) % C

            @pl.when(jnp.logical_not((row == r) & (col == c)))
            def _():
                greet(row, col)

    own = jnp.where(home == c, 1, 0)
    pl.semaphore_wait(barrier, (R - 1) + (C - 1) + 2 * R - 2 * own)

    def right_copy(t):
        return pltpu.make_async_remote_copy(
            src_ref=right_ref, dst_ref=right_buf.at[r],
            send_sem=s_right.at[t], recv_sem=r_right.at[r],
            device_id=((r + t) % R, c), device_id_type=MESH)

    def left_copy(h, t):
        return pltpu.make_async_remote_copy(
            src_ref=left_ref.at[h], dst_ref=left_buf.at[r],
            send_sem=s_left.at[h, t], recv_sem=r_left.at[r],
            device_id=(c * ratio + h, (c + t) % C), device_id_type=MESH)

    def norm_copy(t):
        return pltpu.make_async_remote_copy(
            src_ref=normed_ref, dst_ref=normed_buf.at[c],
            send_sem=s_norm.at[t], recv_sem=r_norm.at[c],
            device_id=(r, (c + t) % C), device_id_type=MESH)

    def logit_copy(k, t):
        return pltpu.make_async_remote_copy(
            src_ref=logit_send.at[k], dst_ref=logit_buf.at[r % ratio, c, k],
            send_sem=s_logit.at[k, t], recv_sem=r_logit.at[r % ratio, c, k],
            device_id=((r + t) % R, home), device_id_type=MESH)

    for h in range(ratio):
        for t in range(C):
            mine = (c * ratio + h == r) & (t == 0)

            @pl.when(jnp.logical_not(mine))
            def _():
                left_copy(h, t).start()

            @pl.when(mine)
            def _():
                left_buf[r] = left_ref[h]

    for t in range(1, R):
        right_copy(t).start()
    for t in range(1, C):
        norm_copy(t).start()
    right_buf[r] = right_ref[...]
    normed_buf[c] = normed_ref[...]

    def wait_left(src):
        pltpu.make_async_remote_copy(
            src_ref=left_ref.at[0], dst_ref=left_buf.at[src],
            send_sem=s_left.at[0, 0], recv_sem=r_left.at[src],
            device_id=(src, home), device_id_type=MESH).wait_recv()

    def wait_right(src):
        pltpu.make_async_remote_copy(
            src_ref=right_ref, dst_ref=right_buf.at[src],
            send_sem=s_right.at[0], recv_sem=r_right.at[src],
            device_id=(src, c), device_id_type=MESH).wait_recv()

    def wait_norm(src):
        pltpu.make_async_remote_copy(
            src_ref=normed_ref, dst_ref=normed_buf.at[src],
            send_sem=s_norm.at[0], recv_sem=r_norm.at[src],
            device_id=(r, src), device_id_type=MESH).wait_recv()

    groups = gates.shape[1] // (heads * LANES)
    group_width = width // groups
    for g in range(groups):
        part = jnp.dot(
            normed_ref[:, g * group_width:(g + 1) * group_width], gate_w_ref[...],
            preferred_element_type=F32)
        for h in range(heads):
            at = (h * groups + g) * LANES
            gates[:, at:at + LANES] = jax.nn.sigmoid(part[:, h * LANES:(h + 1) * LANES])
    values[...] = jnp.zeros_like(values)
    logit_send[...] = jnp.zeros_like(logit_send)

    for src in range(R):
        @pl.when(jnp.logical_not((src == r) & (home == c)))
        def _():
            wait_left(src)

    left_t = left_buf[...].astype(F32).reshape(R * left_buf.shape[1], left_buf.shape[2]).T
    left_all[...] = left_t.astype(BF16)
    for t in range(1, R):
        wait_right((r + t) % R)
    right_all[...] = right_buf[...].astype(F32).reshape(right_all.shape).astype(BF16)

    inverse = 1.0 / jnp.maximum(seqs_ref[0].astype(F32), 1.0)
    ch = product.shape[1] // (right_all.shape[1] // LANES)

    def send_logits(k):
        for t in range(R):
            if t > 0:
                logit_copy(k, t).start()
            else:
                @pl.when(home == c)
                def _():
                    logit_buf[r % ratio, c, k] = logit_send[k]

                @pl.when(home != c)
                def _():
                    logit_copy(k, 0).start()

    def outer_step(k, carry):
        @pl.when(k > 0)
        def _():
            send_logits(k - 1)

        lhs = left_all[pl.ds(pl.multiple_of(k * 8 * ch, 8 * ch), 8 * ch), :]
        for d in range(0, right_all.shape[1] // LANES, 2):
            p = jnp.dot(lhs, right_all[:, d * LANES:(d + 2) * LANES], preferred_element_type=F32)
            p = (p * inverse).astype(BF16)
            for e in range(2):
                product[:, (d + e) * ch:(d + e + 1) * ch, :] = p[
                    :, e * LANES:(e + 1) * LANES].reshape(8, ch, LANES)
        for q in range(0, 8, 2):
            both = jnp.concatenate([product[q], product[q + 1]], axis=1)
            update = jnp.dot(outer_w_ref[...], both, preferred_element_type=F32)
            for e in range(2):
                i = k * 8 + q + e
                step = update[:, e * LANES:(e + 1) * LANES].T[:cols]
                pair = (pair_ref[i].astype(F32) + step).astype(BF16)
                pair_new[i] = pair
                normed = standardize_features(pair).astype(BF16)
                pair_normed[i] = normed
                logits = lax.dot_general(
                    logit_w_ref[...], normed, (((1,), (1,)), ((), ())),
                    preferred_element_type=F32)
                logit_send[k, :, q + e, 0:cols] = logits
        return carry

    lax.fori_loop(0, chunks, outer_step, 0)
    send_logits(chunks - 1)

    trans = down_ref.shape[0]

    def transition_step(k, carry):
        normed = pair_normed[pl.ds(k * 4, 4)].reshape(4 * cols, LANES)
        hidden = jnp.dot(normed, up_ref[...], preferred_element_type=F32)
        front, back = hidden[:, :trans], hidden[:, trans:]
        active = (front / (1.0 + jnp.exp(-front)) * back).astype(BF16)
        update = jnp.dot(active, down_ref[...], preferred_element_type=F32)
        pair = pair_new[pl.ds(k * 4, 4)].astype(F32) + update.reshape(4, cols, LANES)
        out_ref[pl.ds(k * 4, 4)] = pair.astype(BF16)
        return carry

    lax.fori_loop(0, rows // 4, transition_step, 0)

    for t in range(1, C):
        wait_norm((c + t) % C)
    for src in range(C):
        for g in range(groups):
            part = jnp.dot(
                normed_buf[src, :, g * group_width:(g + 1) * group_width], value_w_ref[...],
                preferred_element_type=F32).astype(BF16)
            for h in range(heads):
                at = (h * groups + g) * LANES
                values[src * LANES:src * LANES + cols, at:at + LANES] = part[
                    :, h * LANES:(h + 1) * LANES]

    for h in range(ratio):
        for src in range(C):
            @pl.when(jnp.logical_not((c * ratio + h == r) & (src == c)))
            def _():
                for k in range(chunks):
                    pltpu.make_async_remote_copy(
                        src_ref=logit_send.at[k], dst_ref=logit_buf.at[h, src, k],
                        send_sem=s_logit.at[k, 0], recv_sem=r_logit.at[h, src, k],
                        device_id=(r, home), device_id_type=MESH).wait_recv()

    lane = lax.broadcasted_iota(jnp.int32, (cols, C * LANES), 1)
    valid = (lane % LANES < cols) & (lane // LANES * cols + lane % LANES < length_ref[0])
    span = groups * LANES
    for h in range(heads):
        logits = jnp.concatenate([
            jnp.concatenate(
                [logit_buf[half, src, :, h].reshape(rows, LANES) for src in range(C)], axis=1)
            for half in range(ratio)], axis=0)
        logits = jnp.where(valid, logits, MASKED)
        expo = jnp.exp(logits - jnp.max(logits, axis=1, keepdims=True))
        weights = (expo / jnp.sum(expo, axis=1, keepdims=True)).astype(BF16)
        mean = jnp.dot(weights, values[:, h * span:(h + 1) * span], preferred_element_type=F32)
        mixed = (gates[:, h * span:(h + 1) * span] * mean).astype(BF16)
        for g in range(groups):
            at = (g * heads + h) * LANES
            gated[:, at:at + LANES] = mixed[:, g * LANES:(g + 1) * LANES]
    for g in range(groups):
        part = jnp.dot(
            gated[:, g * heads * LANES:(g + 1) * heads * LANES], final_w_ref[...],
            preferred_element_type=F32)
        sl = slice(g * group_width, (g + 1) * group_width)
        msa_ref[:, sl] = (homolog_ref[:, sl].astype(F32) + part).astype(BF16)

    for t in range(1, R):
        right_copy(t).wait_send()
    for t in range(1, C):
        norm_copy(t).wait_send()
    for h in range(ratio):
        for t in range(C):
            @pl.when(jnp.logical_not((c * ratio + h == r) & (t == 0)))
            def _():
                left_copy(h, t).wait_send()

    def finish(k, carry):
        for t in range(1, R):
            logit_copy(k, t).wait_send()

        @pl.when(home != c)
        def _():
            logit_copy(k, 0).wait_send()

        return carry

    lax.fori_loop(0, chunks, finish, 0)


def local(
    R,
    C,
    homolog_matrix,
    contact_matrix,
    genuine_homolog_total,
    genuine_chain_length,
    tensor_product_matrices,
    tensor_product_final,
    mixing_value_gate_matrix,
    mixing_logit_matrix,
    mixing_final_matrix,
    feedforward_gate_expand,
    feedforward_shrink_matrix,
):
    seqs, cols, feats = homolog_matrix.shape
    rows, _, pair_width = contact_matrix.shape
    ch = tensor_product_matrices.shape[2] // 2
    heads = mixing_logit_matrix.shape[2]
    hidden = mixing_final_matrix.shape[1]
    head_width = hidden // heads
    ratio = R // C
    chunks = rows // 8
    pack = LANES // head_width
    groups = seqs // pack
    r = lax.axis_index("row")
    c = lax.axis_index("col")
    seq_ids = r * seqs + jnp.arange(seqs, dtype=jnp.int32)
    res_ids = c * cols + jnp.arange(cols, dtype=jnp.int32)
    seq_float = (seq_ids < genuine_homolog_total[0]).astype(F32)
    res_float = (res_ids < genuine_chain_length[0]).astype(F32)
    flipped = homolog_matrix.transpose(1, 0, 2)
    normed = standardize_features(homolog_matrix).astype(BF16)
    normed_flat = normed.transpose(1, 0, 2).reshape(cols, seqs * feats)
    left_w = tensor_product_matrices[0][:, :ch]
    right_w = tensor_product_matrices[0][:, ch:]
    right = jnp.einsum("sjf,fd->sdj", normed, right_w, preferred_element_type=F32)
    right = (right * (seq_float[:, None, None] * res_float[None, None, :])).astype(BF16)
    right = jnp.pad(right, ((0, 0), (0, 0), (0, LANES - cols))).reshape(seqs, ch * LANES)
    left = jnp.einsum("sjf,fc->sjc", normed, left_w, preferred_element_type=F32)
    left = (left * (seq_float[:, None, None] * res_float[None, :, None])).astype(BF16)
    left = left.reshape(seqs, ratio, rows * ch).transpose(1, 0, 2)
    outer_w = tensor_product_final[0].reshape(ch, ch, pair_width).transpose(2, 1, 0)
    outer_w = outer_w.reshape(pair_width, ch * ch)
    same = jnp.eye(pack, dtype=BF16)
    vg = mixing_value_gate_matrix[0].reshape(feats, 2, heads, head_width)
    spread = vg[None, :, :, :, None, :] * same[:, None, None, None, :, None]
    spread = spread.reshape(pack * feats, 2, heads * LANES)
    final = mixing_final_matrix[0].reshape(heads, 1, head_width, 1, feats)
    final = (final * same[None, :, None, :, None]).reshape(heads * LANES, pack * feats)
    dims = (R, C, ratio, rows, cols, seqs * feats, heads, chunks)
    vmem = pl.BlockSpec(memory_space=pltpu.VMEM)
    smem = pl.BlockSpec(memory_space=pltpu.SMEM)
    dma = pltpu.SemaphoreType.DMA
    msa, pair_out = pl.pallas_call(
        functools.partial(kernel, dims),
        out_shape=(
            jax.ShapeDtypeStruct((cols, seqs * feats), BF16),
            jax.ShapeDtypeStruct(contact_matrix.shape, BF16),
        ),
        in_specs=[smem] * 2 + [vmem] * 12,
        out_specs=(vmem, vmem),
        scratch_shapes=[
            pltpu.VMEM((R, seqs, ch * LANES), BF16),
            pltpu.VMEM((R, seqs, rows * ch), BF16),
            pltpu.VMEM((C, cols, seqs * feats), BF16),
            pltpu.VMEM((chunks, heads, 8, LANES), F32),
            pltpu.VMEM((ratio, C, chunks, heads, 8, LANES), F32),
            pltpu.VMEM((R * seqs, ch * LANES), BF16),
            pltpu.VMEM((rows * ch, R * seqs), BF16),
            pltpu.VMEM((8, ch * ch, LANES), BF16),
            pltpu.VMEM((rows, cols, pair_width), BF16),
            pltpu.VMEM((rows, cols, pair_width), BF16),
            pltpu.VMEM((C * LANES, heads * groups * LANES), BF16),
            pltpu.VMEM((cols, heads * groups * LANES), F32),
            pltpu.VMEM((cols, heads * groups * LANES), BF16),
            dma((R,)), dma((R,)), dma((ratio, C)), dma((R,)), dma((C,)), dma((C,)),
            dma((chunks, R)), dma((ratio, C, chunks)),
        ],
        compiler_params=pltpu.CompilerParams(
            collective_id=0, has_side_effects=True, vmem_limit_bytes=60 * 1024 * 1024
        ),
        name="msa_block",
    )(
        genuine_homolog_total, genuine_chain_length,
        right, left, normed_flat, flipped.reshape(cols, seqs * feats), contact_matrix,
        outer_w, spread[:, 0], spread[:, 1], mixing_logit_matrix[0].T, final,
        feedforward_gate_expand[0], feedforward_shrink_matrix[0],
    )
    return (msa.reshape(cols, seqs, feats).transpose(1, 0, 2), pair_out)


def solution(mesh):
    in_specs = (P("row", "col", None), P("row", "col", None)) + (P(),) * 9
    out_specs = (P("row", "col", None), P("row", "col", None))
    body = functools.partial(local, mesh.shape["row"], mesh.shape["col"])
    return jax.shard_map(body, mesh=mesh, in_specs=in_specs, out_specs=out_specs, check_vma=False)
```

time: 228 us -> 87.1 us (0.38)
  the two profiles are of different devices: /device:TPU:0 before, /device:TPU:25 now
where the time goes in v1:
time: 87.1 us; the launch traced here: 86.7 us
  Pallas kernels  64.9 us (75%)
  local copies, waits for them, and re-layouts  15.9 us (18%)
  other arithmetic  3.52 us (4%)
  between operations  2.17 us (2%)
    pallas_call x1, Pallas kernels, local(): pl.pallas_call(functools.partial(kernel, dims), out_shape=(jax.ShapeDtype...  64.9 us
    unnamed x15, local copies, waits for them, and re-layouts  4.61 us
    mul x6, local copies, waits for them, and re-layouts, local(): spread = vg[None, :, :, :, None, :] * same[:, None, None, None, :, None]  4.24 us

profile of v1, /device:TPU:25, one launch (start us, length us, event | category | flops | bytes accessed | tf_op | source)
XLA Modules:
  0.0 86.7 jit_solution(5768133891573964941)
XLA Ops:
  0.6 0.0 copy-start
  0.6 0.0 copy-start.1
  0.7 0.0 copy-start.2
  2.0 0.9 %convert_reduce_fusion = f32[8,80]{1,0:T(8,128)S(1)} fusion(bf16[8,80,64]{1,2,0:T(8,128)(2,1)} %param.11), kind=kLoop, calls=%fused_computation.10 | loop fusion | flops 81280 | bytes 84480 | tf_op jit(solution)/shard_map/reduce_sum | solution.py:20
  3.0 1.0 %fusion.5 = f32[8,80]{1,0:T(8,128)S(1)} fusion(bf16[8,80,64]{1,2,0:T(8,128)(2,1)} %param.11, f32[8,80]{1,0:T(8,128)S(1)} %broadcast_multiply_fusion.3), kind=kLoop, calls=%fused_computation.13 | loop fusion | flops 163200 | bytes 87040 | tf_op jit(solution)/shard_map/reduce_sum | solution.py:21
  3.9 0.9 %fusion.6 = bf16[8,80,64]{1,2,0:T(8,128)(2,1)S(1)} fusion(bf16[8,80,64]{1,2,0:T(8,128)(2,1)} %param.11, f32[8,80]{1,0:T(8,128)S(1)} %add_rsqrt_fusion, f32[8,80]{1,0:T(8,128)S(1)} %broadcast_multiply_fusion.3), kind=kLoop, calls=%fused_computation.14 | loop fusion | flops 163840 | bytes 168960 | tf_op jit(solution)/shard_map/convert_element_type | solution.py:312
  4.9 0.1 broadcast_multiply_fusion.2
  5.0 0.8 copy.32
  5.8 0.2 fusion.2
  6.0 0.7 copy.50
  6.6 0.1 fusion.1
  6.8 0.1 copy.33
  6.9 0.2 reshape.140
  7.1 0.6 copy.51
  7.7 0.7 copy.45.normed_ref
  8.4 0.0 copy-done
  8.5 0.7 copy.46.homolog_ref
  9.2 0.0 copy-done.1
  9.2 0.1 copy.37
  9.3 0.8 copy.43.outer_w_ref
  10.1 0.0 copy-done.2
  10.1 0.1 copy.38
  10.3 1.0 %mul.115 = bf16[4,64,2,8,4,32]{1,0,5,4,3,2:T(4,128)(2,1)S(1)} broadcast(bf16[64,2,8,32]{0,3,2,1:T(8,128)(2,1)S(1)} %bitcast.53), dimensions={1,2,3,5} | broadcast | bytes 1114112 | tf_op jit(solution)/shard_map/mul | solution.py:326
  11.3 1.4 %mul.116 = bf16[256,2,1024]{0,2,1:T(8,128)(2,1)S(1)} reshape(bf16[4,64,2,8,4,32]{1,0,5,4,3,2:T(4,128)(2,1)S(1)} %mul.115) | data formatting | bytes 2097152 | tf_op jit(solution)/shard_map/mul | solution.py:326
  12.6 0.5 copy.40
  13.2 0.5 mul.117
  13.7 0.7 mul.118
  14.3 0.2 copy.39
  14.6 0.0 copy-start.3
  14.6 0.1 broadcast_multiply_fusion.1
  14.7 1.0 %slice_bitcast_fusion = (bf16[256,1024]{1,0:T(8,128)(2,1)}, bf16[256,1024]{1,0:T(8,128)(2,1)}) fusion(bf16[256,2,1024]{2,0,1:T(8,128)(2,1)S(1)} %broadcast_multiply_fusion.1), kind=kLoop, calls=%fused_computation.5 | loop fusion | bytes 2097152 | tf_op jit(solution)/shard_map/squeeze | solution.py:366
  15.7 0.1 copy.42
  15.8 0.0 copy-done.3
  15.8 0.1 copy.41
  16.0 0.5 broadcast_multiply_fusion
  16.4 1.5 %mul.125.final_w_ref = bf16[1024,256]{1,0:T(8,128)(2,1)} reshape(bf16[8,4,32,4,64]{4,3,2,1,0:T(4,128)(2,1)S(1)} %broadcast_multiply_fusion) | data formatting | bytes 1048576 | tf_op jit(solution)/shard_map/mul | solution.py:329
  17.9 64.9 %msa_block.1 = (bf16[80,512]{1,0:T(8,128)(2,1)}, bf16[40,80,128]{2,1,0:T(8,128)(2,1)}) custom-call(s32[1]{0:T(128)} %copy.53.seqs_ref, s32[1]{0:T(128)} %copy.54.length_ref, bf16[8,4096]{1,0:T(8,128)(2,1)} %bitcast.54, bf16[2,8,1280]{2,1,0:T(8,128)(2,1)} %bitcast.58, bf16[80,512]{1,0:T(8,128)(2,1)} %copy.45.normed_ref, bf16[80,512]{1,0:T(8,128)(2,1)} %copy.46.homolog_ref, ...), custom_call_target="tpu_custom_call" | custom-call | tf_op jit(solution)/shard_map/msa_block/pallas_call | solution.py:334
  82.8 1.0 %reshape.144 = bf16[80,8,64]{2,1,0:T(8,128)(2,1)S(1)} reshape(bf16[80,512]{1,0:T(8,128)(2,1)} %get-tuple-element.4) | data formatting | bytes 163840 | tf_op jit(solution)/shard_map/reshape | solution.py:369
  83.8 0.8 copy.44
  84.7 2.1 %copy.55 = bf16[40,80,128]{2,1,0:T(8,128)(2,1)} copy(bf16[40,80,128]{2,1,0:T(8,128)(2,1)} %get-tuple-element.15) | data formatting | bytes 1638400
  (6 shorter events, 0.0 us)
Async XLA Ops:
  0.6 7.8 %copy-start = (bf16[8,80,64]{1,2,0:T(8,128)(2,1)S(1)}, bf16[8,80,64]{1,2,0:T(8,128)(2,1)}, u32[]{:S(2)}) copy-start(bf16[8,80,64]{1,2,0:T(8,128)(2,1)} %param.11) | copy-start | bytes 245764
  0.6 8.5 %copy-start.1 = (bf16[1,1024,128]{2,1,0:T(8,128)(2,1)S(1)}, bf16[1,1024,128]{2,1,0:T(8,128)(2,1)}, u32[]{:S(2)}) copy-start(bf16[1,1024,128]{2,1,0:T(8,128)(2,1)} %param.16) | copy-start | bytes 786436
  0.7 9.5 %copy-start.2 = (bf16[1,64,512]{2,1,0:T(8,128)(2,1)S(1)}, bf16[1,64,512]{2,1,0:T(8,128)(2,1)}, u32[]{:S(2)}) copy-start(bf16[1,64,512]{2,1,0:T(8,128)(2,1)} %param.17) | copy-start | bytes 196612
  14.6 1.3 %copy-start.3 = (bf16[1,256,64]{1,2,0:T(8,128)(2,1)S(1)}, bf16[1,256,64]{1,2,0:T(8,128)(2,1)}, u32[]{:S(2)}) copy-start(bf16[1,256,64]{1,2,0:T(8,128)(2,1)} %param.19) | copy-start | bytes 98308

commit v2 on v1

--- a/solution.py
+++ b/solution.py
@@ -22,15 +22,24 @@
     return center * lax.rsqrt(spread + EPSILON)
 
 
+def flip(index, mask):
+    bit = 1
+    while bit <= mask:
+        if mask & bit:
+            index = index + bit - 2 * bit * ((index // bit) % 2)
+        bit *= 2
+    return index
+
+
 def kernel(
     dims,
     seqs_ref, length_ref,
     right_ref, left_ref, normed_ref, homolog_ref, pair_ref,
     outer_w_ref, value_w_ref, gate_w_ref, logit_w_ref, final_w_ref, up_ref, down_ref,
     msa_ref, out_ref,
-    right_buf, left_buf, normed_buf, logit_send, logit_buf,
+    right_buf, left_buf, normed_buf, logit_send, logit_buf, weight_buf,
     right_all, left_all, product, pair_new, pair_normed, values, gates, gated,
-    s_right, r_right, s_left, r_left, s_norm, r_norm, s_logit, r_logit,
+    s_right, r_right, s_left, r_left, s_norm, r_norm, s_logit, r_logit, s_weight, r_weight,
 ):
     R, C, ratio, rows, cols, width, heads, chunks = dims
     r = lax.axis_index("row")
@@ -64,11 +73,13 @@
     own = jnp.where(home == c, 1, 0)
     pl.semaphore_wait(barrier, (R - 1) + (C - 1) + 2 * R - 2 * own)
 
-    def right_copy(t):
+    def right_copy(n):
+        root = flip(r, n & (n - 1))
         return pltpu.make_async_remote_copy(
-            src_ref=right_ref, dst_ref=right_buf.at[r],
-            send_sem=s_right.at[t], recv_sem=r_right.at[r],
-            device_id=((r + t) % R, c), device_id_type=MESH)
+            src_ref=right_buf.at[root] if n & (n - 1) else right_ref,
+            dst_ref=right_buf.at[root],
+            send_sem=s_right.at[n], recv_sem=r_right.at[n],
+            device_id=(flip(r, n & -n), c), device_id_type=MESH)
 
     def left_copy(h, t):
         return pltpu.make_async_remote_copy(
@@ -82,11 +93,26 @@
             send_sem=s_norm.at[t], recv_sem=r_norm.at[c],
             device_id=(r, (c + t) % C), device_id_type=MESH)
 
-    def logit_copy(k, t):
+    def logit_copy(k):
         return pltpu.make_async_remote_copy(
-            src_ref=logit_send.at[k], dst_ref=logit_buf.at[r % ratio, c, k],
-            send_sem=s_logit.at[k, t], recv_sem=r_logit.at[r % ratio, c, k],
-            device_id=((r + t) % R, home), device_id_type=MESH)
+            src_ref=logit_send.at[k], dst_ref=logit_buf.at[c, k],
+            send_sem=s_logit.at[k], recv_sem=r_logit.at[c, k],
+            device_id=(r, home), device_id_type=MESH)
+
+    steps = [R >> (e + 1) for e in range(R.bit_length() - 1)]
+
+    def weight_copy(half, p, e):
+        return pltpu.make_async_remote_copy(
+            src_ref=weight_buf.at[half, p], dst_ref=weight_buf.at[half, p],
+            send_sem=s_weight.at[half, p, e], recv_sem=r_weight.at[half, p],
+            device_id=(flip(r, steps[e]), c), device_id_type=MESH)
+
+    def relation(half):
+        root = c * ratio + half
+        total = 0
+        for bit in steps:
+            total = total + bit * (((r // bit) % 2 + (root // bit) % 2) % 2)
+        return total
 
     for h in range(ratio):
         for t in range(C):
@@ -100,8 +126,8 @@
             def _():
                 left_buf[r] = left_ref[h]
 
-    for t in range(1, R):
-        right_copy(t).start()
+    for bit in steps:
+        right_copy(bit).start()
     for t in range(1, C):
         norm_copy(t).start()
     right_buf[r] = right_ref[...]
@@ -113,17 +139,23 @@
             send_sem=s_left.at[0, 0], recv_sem=r_left.at[src],
             device_id=(src, home), device_id_type=MESH).wait_recv()
 
-    def wait_right(src):
+    def wait_right(n):
         pltpu.make_async_remote_copy(
-            src_ref=right_ref, dst_ref=right_buf.at[src],
-            send_sem=s_right.at[0], recv_sem=r_right.at[src],
-            device_id=(src, c), device_id_type=MESH).wait_recv()
+            src_ref=right_ref, dst_ref=right_buf.at[flip(r, n)],
+            send_sem=s_right.at[n], recv_sem=r_right.at[n],
+            device_id=(flip(r, n & -n), c), device_id_type=MESH).wait_recv()
 
     def wait_norm(src):
         pltpu.make_async_remote_copy(
             src_ref=normed_ref, dst_ref=normed_buf.at[src],
             send_sem=s_norm.at[0], recv_sem=r_norm.at[src],
             device_id=(r, src), device_id_type=MESH).wait_recv()
+
+    for n in sorted(range(1, R), key=lambda n: (bin(n).count("1"), -(n & -n))):
+        wait_right(n)
+        for bit in steps:
+            if bit < n & -n:
+                right_copy(n + bit).start()
 
     groups = gates.shape[1] // (heads * LANES)
     group_width = width // groups
@@ -144,25 +176,19 @@
 
     left_t = left_buf[...].astype(F32).reshape(R * left_buf.shape[1], left_buf.shape[2]).T
     left_all[...] = left_t.astype(BF16)
-    for t in range(1, R):
-        wait_right((r + t) % R)
     right_all[...] = right_buf[...].astype(F32).reshape(right_all.shape).astype(BF16)
 
     inverse = 1.0 / jnp.maximum(seqs_ref[0].astype(F32), 1.0)
     ch = product.shape[1] // (right_all.shape[1] // LANES)
 
     def send_logits(k):
-        for t in range(R):
-            if t > 0:
-                logit_copy(k, t).start()
-            else:
-                @pl.when(home == c)
-                def _():
-                    logit_buf[r % ratio, c, k] = logit_send[k]
-
-                @pl.when(home != c)
-                def _():
-                    logit_copy(k, 0).start()
+        @pl.when(home == c)
+        def _():
+            logit_buf[c, k] = logit_send[k]
+
+        @pl.when(home != c)
+        def _():
+            logit_copy(k).start()
 
     def outer_step(k, carry):
         @pl.when(k > 0)
@@ -207,7 +233,38 @@
         out_ref[pl.ds(k * 4, 4)] = pair.astype(BF16)
         return carry
 
-    lax.fori_loop(0, rows // 4, transition_step, 0)
+    lax.fori_loop(0, rows // 8, transition_step, 0)
+
+    pieces = weight_buf.shape[1]
+    per = heads // pieces
+
+    @pl.when(home == c)
+    def _():
+        for src in range(C):
+            @pl.when(src != c)
+            def _():
+                for k in range(chunks):
+                    pltpu.make_async_remote_copy(
+                        src_ref=logit_send.at[k], dst_ref=logit_buf.at[src, k],
+                        send_sem=s_logit.at[k], recv_sem=r_logit.at[src, k],
+                        device_id=(r, src), device_id_type=MESH).wait_recv()
+
+        lane = lax.broadcasted_iota(jnp.int32, (rows, C * LANES), 1)
+        valid = (lane % LANES < cols) & (
+            lane // LANES * cols + lane % LANES < length_ref[0])
+        for h in range(heads):
+            logits = jnp.concatenate(
+                [logit_buf[src, :, h].reshape(rows, LANES) for src in range(C)], axis=1)
+            logits = jnp.where(valid, logits, MASKED)
+            expo = jnp.exp(logits - jnp.max(logits, axis=1, keepdims=True))
+            weights = expo / jnp.sum(expo, axis=1, keepdims=True)
+            weight_buf[r % ratio, h // per, h % per] = weights.astype(BF16)
+
+        for p in range(pieces):
+            for e in range(len(steps)):
+                weight_copy(r % ratio, p, e).start()
+
+    lax.fori_loop(rows // 8, rows // 4, transition_step, 0)
 
     for t in range(1, C):
         wait_norm((c + t) % C)
@@ -221,27 +278,23 @@
                 values[src * LANES:src * LANES + cols, at:at + LANES] = part[
                     :, h * LANES:(h + 1) * LANES]
 
-    for h in range(ratio):
-        for src in range(C):
-            @pl.when(jnp.logical_not((c * ratio + h == r) & (src == c)))
-            def _():
-                for k in range(chunks):
-                    pltpu.make_async_remote_copy(
-                        src_ref=logit_send.at[k], dst_ref=logit_buf.at[h, src, k],
-                        send_sem=s_logit.at[k, 0], recv_sem=r_logit.at[h, src, k],
-                        device_id=(r, home), device_id_type=MESH).wait_recv()
-
-    lane = lax.broadcasted_iota(jnp.int32, (cols, C * LANES), 1)
-    valid = (lane % LANES < cols) & (lane // LANES * cols + lane % LANES < length_ref[0])
+    for p in range(pieces):
+        for half in range(ratio):
+            rel = relation(half)
+
+            @pl.when(rel != 0)
+            def _():
+                weight_copy(half, p, 0).wait_recv()
+                for e, bit in enumerate(steps):
+                    @pl.when(rel % (2 * bit) == 0)
+                    def _():
+                        weight_copy(half, p, e).start()
+
     span = groups * LANES
     for h in range(heads):
-        logits = jnp.concatenate([
-            jnp.concatenate(
-                [logit_buf[half, src, :, h].reshape(rows, LANES) for src in range(C)], axis=1)
-            for half in range(ratio)], axis=0)
-        logits = jnp.where(valid, logits, MASKED)
-        expo = jnp.exp(logits - jnp.max(logits, axis=1, keepdims=True))
-        weights = (expo / jnp.sum(expo, axis=1, keepdims=True)).astype(BF16)
+        weights = jnp.concatenate(
+            [weight_buf[half, h // per, h % per].astype(F32) for half in range(ratio)],
+            axis=0).astype(BF16)
         mean = jnp.dot(weights, values[:, h * span:(h + 1) * span], preferred_element_type=F32)
         mixed = (gates[:, h * span:(h + 1) * span] * mean).astype(BF16)
         for g in range(groups):
@@ -264,17 +317,18 @@
             def _():
                 left_copy(h, t).wait_send()
 
-    def finish(k, carry):
-        for t in range(1, R):
-            logit_copy(k, t).wait_send()
-
-        @pl.when(home != c)
-        def _():
-            logit_copy(k, 0).wait_send()
-
-        return carry
-
-    lax.fori_loop(0, chunks, finish, 0)
+    @pl.when(home != c)
+    def _():
+        for k in range(chunks):
+            logit_copy(k).wait_send()
+
+    for p in range(pieces):
+        for half in range(ratio):
+            rel = relation(half)
+            for e, bit in enumerate(steps):
+                @pl.when(rel % (2 * bit) == 0)
+                def _():
+                    weight_copy(half, p, e).wait_send()
 
 
 def local(
@@ -344,7 +398,8 @@
             pltpu.VMEM((R, seqs, rows * ch), BF16),
             pltpu.VMEM((C, cols, seqs * feats), BF16),
             pltpu.VMEM((chunks, heads, 8, LANES), F32),
-            pltpu.VMEM((ratio, C, chunks, heads, 8, LANES), F32),
+            pltpu.VMEM((C, chunks, heads, 8, LANES), F32),
+            pltpu.VMEM((ratio, heads // 2, 2, rows, C * LANES), BF16),
             pltpu.VMEM((R * seqs, ch * LANES), BF16),
             pltpu.VMEM((rows * ch, R * seqs), BF16),
             pltpu.VMEM((8, ch * ch, LANES), BF16),
@@ -354,7 +409,8 @@
             pltpu.VMEM((cols, heads * groups * LANES), F32),
             pltpu.VMEM((cols, heads * groups * LANES), BF16),
             dma((R,)), dma((R,)), dma((ratio, C)), dma((R,)), dma((C,)), dma((C,)),
-            dma((chunks, R)), dma((ratio, C, chunks)),
+            dma((chunks,)), dma((C, chunks)),
+            dma((ratio, heads // 2, R.bit_length())), dma((ratio, heads // 2)),
         ],
         compiler_params=pltpu.CompilerParams(
             collective_id=0, has_side_effects=True, vmem_limit_bytes=60 * 1024 * 1024

time: 87.1 us -> 103 us (1.18)
  the two profiles are of different devices: /device:TPU:25 before, /device:TPU:12 now
where the time goes in v2:
time: 103 us; the launch traced here: 102 us
  Pallas kernels  80.6 us (78%)
  local copies, waits for them, and re-layouts  15.9 us (15%)
  other arithmetic  3.52 us (3%)
  between operations  2.17 us (2%)
    pallas_call x1, Pallas kernels, local(): pl.pallas_call(functools.partial(kernel, dims), out_shape=(jax.ShapeDtype...  80.6 us
    unnamed x15, local copies, waits for them, and re-layouts  4.61 us
    mul x6, local copies, waits for them, and re-layouts, local(): spread = vg[None, :, :, :, None, :] * same[:, None, None, None, :, None]  4.24 us

profile of v2, /device:TPU:12, one launch (start us, length us, event | category | flops | bytes accessed | tf_op | source)
XLA Modules:
  0.0 102.4 jit_solution(11079626565163699807)
XLA Ops:
  0.6 0.0 copy-start
  0.6 0.0 copy-start.1
  0.7 0.0 copy-start.2
  2.0 0.9 convert_reduce_fusion
  3.0 1.0 fusion.5
  3.9 0.9 fusion.6
  4.9 0.1 broadcast_multiply_fusion.2
  5.0 0.8 copy.32
  5.8 0.2 fusion.2
  6.0 0.7 copy.50
  6.6 0.1 fusion.1
  6.8 0.1 copy.33
  6.9 0.2 reshape.140
  7.1 0.6 copy.51
  7.7 0.7 copy.45.normed_ref
  8.5 0.0 copy-done
  8.5 0.7 copy.46.homolog_ref
  9.2 0.0 copy-done.1
  9.2 0.1 copy.37
  9.3 0.8 copy.43.outer_w_ref
  10.1 0.0 copy-done.2
  10.1 0.1 copy.38
  10.3 1.0 mul.115
  11.3 1.4 %mul.116 = bf16[256,2,1024]{0,2,1:T(8,128)(2,1)S(1)} reshape(bf16[4,64,2,8,4,32]{1,0,5,4,3,2:T(4,128)(2,1)S(1)} %mul.115) | data formatting | bytes 2097152 | tf_op jit(solution)/shard_map/mul | solution.py:380
  12.6 0.5 copy.40
  13.2 0.5 mul.117
  13.7 0.7 mul.118
  14.3 0.2 copy.39
  14.6 0.0 copy-start.3
  14.6 0.1 broadcast_multiply_fusion.1
  14.7 1.0 %slice_bitcast_fusion = (bf16[256,1024]{1,0:T(8,128)(2,1)}, bf16[256,1024]{1,0:T(8,128)(2,1)}) fusion(bf16[256,2,1024]{2,0,1:T(8,128)(2,1)S(1)} %broadcast_multiply_fusion.1), kind=kLoop, calls=%fused_computation.5 | loop fusion | bytes 2097152 | tf_op jit(solution)/shard_map/squeeze | solution.py:422
  15.7 0.1 copy.42
  15.8 0.0 copy-done.3
  15.8 0.1 copy.41
  16.0 0.5 broadcast_multiply_fusion
  16.4 1.5 %mul.125.final_w_ref = bf16[1024,256]{1,0:T(8,128)(2,1)} reshape(bf16[8,4,32,4,64]{4,3,2,1,0:T(4,128)(2,1)S(1)} %broadcast_multiply_fusion) | data formatting | bytes 1048576 | tf_op jit(solution)/shard_map/mul | solution.py:383
  17.9 80.6 %msa_block.1 = (bf16[80,512]{1,0:T(8,128)(2,1)}, bf16[40,80,128]{2,1,0:T(8,128)(2,1)}) custom-call(s32[1]{0:T(128)} %copy.53.seqs_ref, s32[1]{0:T(128)} %copy.54.length_ref, bf16[8,4096]{1,0:T(8,128)(2,1)} %bitcast.54, bf16[2,8,1280]{2,1,0:T(8,128)(2,1)} %bitcast.58, bf16[80,512]{1,0:T(8,128)(2,1)} %copy.45.normed_ref, bf16[80,512]{1,0:T(8,128)(2,1)} %copy.46.homolog_ref, ...), custom_call_target="tpu_custom_call" | custom-call | tf_op jit(solution)/shard_map/msa_block/pallas_call | solution.py:388
  98.5 1.0 %reshape.144 = bf16[80,8,64]{2,1,0:T(8,128)(2,1)S(1)} reshape(bf16[80,512]{1,0:T(8,128)(2,1)} %get-tuple-element.4) | data formatting | bytes 163840 | tf_op jit(solution)/shard_map/reshape | solution.py:425
  99.5 0.8 copy.44
  100.3 2.1 %copy.55 = bf16[40,80,128]{2,1,0:T(8,128)(2,1)} copy(bf16[40,80,128]{2,1,0:T(8,128)(2,1)} %get-tuple-element.15) | data formatting | bytes 1638400
  (6 shorter events, 0.0 us)
Async XLA Ops:
  0.6 7.8 %copy-start = (bf16[8,80,64]{1,2,0:T(8,128)(2,1)S(1)}, bf16[8,80,64]{1,2,0:T(8,128)(2,1)}, u32[]{:S(2)}) copy-start(bf16[8,80,64]{1,2,0:T(8,128)(2,1)} %param.11) | copy-start | bytes 245764
  0.6 8.5 %copy-start.1 = (bf16[1,1024,128]{2,1,0:T(8,128)(2,1)S(1)}, bf16[1,1024,128]{2,1,0:T(8,128)(2,1)}, u32[]{:S(2)}) copy-start(bf16[1,1024,128]{2,1,0:T(8,128)(2,1)} %param.16) | copy-start | bytes 786436
  0.7 9.5 %copy-start.2 = (bf16[1,64,512]{2,1,0:T(8,128)(2,1)S(1)}, bf16[1,64,512]{2,1,0:T(8,128)(2,1)}, u32[]{:S(2)}) copy-start(bf16[1,64,512]{2,1,0:T(8,128)(2,1)} %param.17) | copy-start | bytes 196612
  14.6 1.3 %copy-start.3 = (bf16[1,256,64]{1,2,0:T(8,128)(2,1)S(1)}, bf16[1,256,64]{1,2,0:T(8,128)(2,1)}, u32[]{:S(2)}) copy-start(bf16[1,256,64]{1,2,0:T(8,128)(2,1)} %param.19) | copy-start | bytes 98308

commit v3 on v1

--- a/solution.py
+++ b/solution.py
@@ -22,15 +22,24 @@
     return center * lax.rsqrt(spread + EPSILON)
 
 
+def flip(index, mask):
+    bit = 1
+    while bit <= mask:
+        if mask & bit:
+            index = index + bit - 2 * bit * ((index // bit) % 2)
+        bit *= 2
+    return index
+
+
 def kernel(
     dims,
     seqs_ref, length_ref,
     right_ref, left_ref, normed_ref, homolog_ref, pair_ref,
     outer_w_ref, value_w_ref, gate_w_ref, logit_w_ref, final_w_ref, up_ref, down_ref,
     msa_ref, out_ref,
-    right_buf, left_buf, normed_buf, logit_send, logit_buf,
+    right_buf, left_buf, normed_buf, logit_send, logit_buf, stat_send, stat_buf, expo_tile,
     right_all, left_all, product, pair_new, pair_normed, values, gates, gated,
-    s_right, r_right, s_left, r_left, s_norm, r_norm, s_logit, r_logit,
+    s_right, r_right, s_left, r_left, s_norm, r_norm, s_logit, r_logit, s_stat, r_stat,
 ):
     R, C, ratio, rows, cols, width, heads, chunks = dims
     r = lax.axis_index("row")
@@ -64,11 +73,13 @@
     own = jnp.where(home == c, 1, 0)
     pl.semaphore_wait(barrier, (R - 1) + (C - 1) + 2 * R - 2 * own)
 
-    def right_copy(t):
+    def right_copy(n):
+        root = flip(r, n & (n - 1))
         return pltpu.make_async_remote_copy(
-            src_ref=right_ref, dst_ref=right_buf.at[r],
-            send_sem=s_right.at[t], recv_sem=r_right.at[r],
-            device_id=((r + t) % R, c), device_id_type=MESH)
+            src_ref=right_buf.at[root] if n & (n - 1) else right_ref,
+            dst_ref=right_buf.at[root],
+            send_sem=s_right.at[n], recv_sem=r_right.at[n],
+            device_id=(flip(r, n & -n), c), device_id_type=MESH)
 
     def left_copy(h, t):
         return pltpu.make_async_remote_copy(
@@ -88,6 +99,12 @@
             send_sem=s_logit.at[k, t], recv_sem=r_logit.at[r % ratio, c, k],
             device_id=((r + t) % R, home), device_id_type=MESH)
 
+    def stat_copy(t):
+        return pltpu.make_async_remote_copy(
+            src_ref=stat_send, dst_ref=stat_buf.at[r % ratio, c],
+            send_sem=s_stat.at[t], recv_sem=r_stat.at[r % ratio, c],
+            device_id=((r + t) % R, home), device_id_type=MESH)
+
     for h in range(ratio):
         for t in range(C):
             mine = (c * ratio + h == r) & (t == 0)
@@ -100,10 +117,9 @@
             def _():
                 left_buf[r] = left_ref[h]
 
-    for t in range(1, R):
-        right_copy(t).start()
-    for t in range(1, C):
-        norm_copy(t).start()
+    steps = [R >> (e + 1) for e in range(R.bit_length() - 1)]
+    for bit in steps:
+        right_copy(bit).start()
     right_buf[r] = right_ref[...]
     normed_buf[c] = normed_ref[...]
 
@@ -113,17 +129,26 @@
             send_sem=s_left.at[0, 0], recv_sem=r_left.at[src],
             device_id=(src, home), device_id_type=MESH).wait_recv()
 
-    def wait_right(src):
+    def wait_right(n):
         pltpu.make_async_remote_copy(
-            src_ref=right_ref, dst_ref=right_buf.at[src],
-            send_sem=s_right.at[0], recv_sem=r_right.at[src],
-            device_id=(src, c), device_id_type=MESH).wait_recv()
+            src_ref=right_ref, dst_ref=right_buf.at[flip(r, n)],
+            send_sem=s_right.at[n], recv_sem=r_right.at[n],
+            device_id=(flip(r, n & -n), c), device_id_type=MESH).wait_recv()
 
     def wait_norm(src):
         pltpu.make_async_remote_copy(
             src_ref=normed_ref, dst_ref=normed_buf.at[src],
             send_sem=s_norm.at[0], recv_sem=r_norm.at[src],
             device_id=(r, src), device_id_type=MESH).wait_recv()
+
+    for n in sorted(range(1, R), key=lambda n: (bin(n).count("1"), -(n & -n))):
+        wait_right(n)
+        for bit in steps:
+            if bit < n & -n:
+                right_copy(n + bit).start()
+
+    for t in range(1, C):
+        norm_copy(t).start()
 
     groups = gates.shape[1] // (heads * LANES)
     group_width = width // groups
@@ -135,7 +160,7 @@
             at = (h * groups + g) * LANES
             gates[:, at:at + LANES] = jax.nn.sigmoid(part[:, h * LANES:(h + 1) * LANES])
     values[...] = jnp.zeros_like(values)
-    logit_send[...] = jnp.zeros_like(logit_send)
+    stat_send[...] = jnp.zeros_like(stat_send)
 
     for src in range(R):
         @pl.when(jnp.logical_not((src == r) & (home == c)))
@@ -144,9 +169,11 @@
 
     left_t = left_buf[...].astype(F32).reshape(R * left_buf.shape[1], left_buf.shape[2]).T
     left_all[...] = left_t.astype(BF16)
-    for t in range(1, R):
-        wait_right((r + t) % R)
-    right_all[...] = right_buf[...].astype(F32).reshape(right_all.shape).astype(BF16)
+    right_flat = right_buf[...].astype(F32).reshape(right_all.shape[0], right_buf.shape[2])
+    zeros = jnp.zeros((right_all.shape[0], LANES - cols), F32)
+    for d in range(right_buf.shape[2] // cols):
+        right_all[:, d * LANES:(d + 1) * LANES] = jnp.concatenate(
+            [right_flat[:, d * cols:(d + 1) * cols], zeros], axis=1).astype(BF16)
 
     inverse = 1.0 / jnp.maximum(seqs_ref[0].astype(F32), 1.0)
     ch = product.shape[1] // (right_all.shape[1] // LANES)
@@ -163,6 +190,9 @@
                 @pl.when(home != c)
                 def _():
                     logit_copy(k, 0).start()
+
+    row_lane = lax.broadcasted_iota(jnp.int32, (heads, LANES), 1)
+    real = c * cols + lax.broadcasted_iota(jnp.int32, (heads, cols), 1) < length_ref[0]
 
     def outer_step(k, carry):
         @pl.when(k > 0)
@@ -189,11 +219,30 @@
                 logits = lax.dot_general(
                     logit_w_ref[...], normed, (((1,), (1,)), ((), ())),
                     preferred_element_type=F32)
-                logit_send[k, :, q + e, 0:cols] = logits
+                logits = jnp.where(real, logits, MASKED)
+                peak = jnp.max(logits, axis=1, keepdims=True)
+                expo = jnp.exp(logits - peak)
+                expo_tile[:, q + e, 0:cols] = expo
+                stat_send[0] = jnp.where(row_lane == i, peak, stat_send[0])
+                stat_send[1] = jnp.where(
+                    row_lane == i, jnp.sum(expo, axis=1, keepdims=True), stat_send[1])
+        logit_send[k] = jnp.concatenate(
+            [expo_tile[h, :, 0:cols] for h in range(heads)], axis=1).astype(BF16)
         return carry
 
     lax.fori_loop(0, chunks, outer_step, 0)
     send_logits(chunks - 1)
+    for t in range(R):
+        if t > 0:
+            stat_copy(t).start()
+        else:
+            @pl.when(home == c)
+            def _():
+                stat_buf[r % ratio, c] = stat_send[...]
+
+            @pl.when(home != c)
+            def _():
+                stat_copy(0).start()
 
     trans = down_ref.shape[0]
 
@@ -230,18 +279,30 @@
                         src_ref=logit_send.at[k], dst_ref=logit_buf.at[h, src, k],
                         send_sem=s_logit.at[k, 0], recv_sem=r_logit.at[h, src, k],
                         device_id=(r, home), device_id_type=MESH).wait_recv()
-
-    lane = lax.broadcasted_iota(jnp.int32, (cols, C * LANES), 1)
-    valid = (lane % LANES < cols) & (lane // LANES * cols + lane % LANES < length_ref[0])
+                pltpu.make_async_remote_copy(
+                    src_ref=stat_send, dst_ref=stat_buf.at[h, src],
+                    send_sem=s_stat.at[0], recv_sem=r_stat.at[h, src],
+                    device_id=(r, home), device_id_type=MESH).wait_recv()
+
+    scales = []
+    for half in range(ratio):
+        peaks = [stat_buf[half, src, 0] for src in range(C)]
+        top = functools.reduce(jnp.maximum, peaks)
+        shifts = [jnp.exp(peak - top) for peak in peaks]
+        total = sum(shift * stat_buf[half, src, 1] for src, shift in enumerate(shifts))
+        total = jnp.where(row_lane < rows, total, 1.0)
+        scales.append([(shift / total).T for shift in shifts])
+    gap = jnp.zeros((rows, LANES - cols), F32)
+    expos = [[logit_buf[half, src].astype(F32).reshape(rows, heads * cols) for src in range(C)]
+             for half in range(ratio)]
     span = groups * LANES
     for h in range(heads):
-        logits = jnp.concatenate([
-            jnp.concatenate(
-                [logit_buf[half, src, :, h].reshape(rows, LANES) for src in range(C)], axis=1)
-            for half in range(ratio)], axis=0)
-        logits = jnp.where(valid, logits, MASKED)
-        expo = jnp.exp(logits - jnp.max(logits, axis=1, keepdims=True))
-        weights = (expo / jnp.sum(expo, axis=1, keepdims=True)).astype(BF16)
+        weights = jnp.concatenate([
+            jnp.concatenate([
+                piece for src in range(C) for piece in (
+                    expos[half][src][:, h * cols:(h + 1) * cols]
+                    * scales[half][src][:rows, h:h + 1], gap)], axis=1)
+            for half in range(ratio)], axis=0).astype(BF16)
         mean = jnp.dot(weights, values[:, h * span:(h + 1) * span], preferred_element_type=F32)
         mixed = (gates[:, h * span:(h + 1) * span] * mean).astype(BF16)
         for g in range(groups):
@@ -273,6 +334,13 @@
             logit_copy(k, 0).wait_send()
 
         return carry
+
+    for t in range(1, R):
+        stat_copy(t).wait_send()
+
+    @pl.when(home != c)
+    def _():
+        stat_copy(0).wait_send()
 
     lax.fori_loop(0, chunks, finish, 0)
 
@@ -315,7 +383,7 @@
     right_w = tensor_product_matrices[0][:, ch:]
     right = jnp.einsum("sjf,fd->sdj", normed, right_w, preferred_element_type=F32)
     right = (right * (seq_float[:, None, None] * res_float[None, None, :])).astype(BF16)
-    right = jnp.pad(right, ((0, 0), (0, 0), (0, LANES - cols))).reshape(seqs, ch * LANES)
+    right = right.reshape(seqs, ch * cols)
     left = jnp.einsum("sjf,fc->sjc", normed, left_w, preferred_element_type=F32)
     left = (left * (seq_float[:, None, None] * res_float[None, :, None])).astype(BF16)
     left = left.reshape(seqs, ratio, rows * ch).transpose(1, 0, 2)
@@ -340,11 +408,14 @@
         in_specs=[smem] * 2 + [vmem] * 12,
         out_specs=(vmem, vmem),
         scratch_shapes=[
-            pltpu.VMEM((R, seqs, ch * LANES), BF16),
+            pltpu.VMEM((R, seqs, ch * cols), BF16),
             pltpu.VMEM((R, seqs, rows * ch), BF16),
             pltpu.VMEM((C, cols, seqs * feats), BF16),
-            pltpu.VMEM((chunks, heads, 8, LANES), F32),
-            pltpu.VMEM((ratio, C, chunks, heads, 8, LANES), F32),
+            pltpu.VMEM((chunks, 8, heads * cols), BF16),
+            pltpu.VMEM((ratio, C, chunks, 8, heads * cols), BF16),
+            pltpu.VMEM((2, heads, LANES), F32),
+            pltpu.VMEM((ratio, C, 2, heads, LANES), F32),
+            pltpu.VMEM((heads, 8, LANES), F32),
             pltpu.VMEM((R * seqs, ch * LANES), BF16),
             pltpu.VMEM((rows * ch, R * seqs), BF16),
             pltpu.VMEM((8, ch * ch, LANES), BF16),
@@ -354,7 +425,7 @@
             pltpu.VMEM((cols, heads * groups * LANES), F32),
             pltpu.VMEM((cols, heads * groups * LANES), BF16),
             dma((R,)), dma((R,)), dma((ratio, C)), dma((R,)), dma((C,)), dma((C,)),
-            dma((chunks, R)), dma((ratio, C, chunks)),
+            dma((chunks, R)), dma((ratio, C, chunks)), dma((R,)), dma((ratio, C)),
         ],
         compiler_params=pltpu.CompilerParams(
             collective_id=0, has_side_effects=True, vmem_limit_bytes=60 * 1024 * 1024

time: 87.1 us -> 72.3 us (0.83)
  the two profiles are of different devices: /device:TPU:25 before, /device:TPU:0 now
where the time goes in v3:
time: 72.3 us; the launch traced here: 71.9 us
  Pallas kernels  49 us (68%)
  local copies, waits for them, and re-layouts  16.9 us (23%)
  other arithmetic  3.52 us (5%)
  between operations  2.15 us (3%)
    pallas_call x1, Pallas kernels, local(): pl.pallas_call(functools.partial(kernel, dims), out_shape=(jax.ShapeDtype...  49 us
    mul x6, local copies, waits for them, and re-layouts, local(): spread = vg[None, :, :, :, None, :] * same[:, None, None, None, :, None]  4.24 us
    unnamed x11, local copies, waits for them, and re-layouts  3.94 us
    reshape x1, local copies, waits for them, and re-layouts, local(): flipped.reshape(cols, seqs * feats)  1.64 us
    mul x1, local copies, waits for them, and re-layouts, local(): final * same[None, :, None, :, None]  1.49 us

profile of v3, /device:TPU:0, one launch (start us, length us, event | category | flops | bytes accessed | tf_op | source)
XLA Modules:
  0.0 71.9 jit_solution(5671568309091319935)
XLA Ops:
  0.6 0.0 copy-start
  0.6 0.0 copy-start.1
  2.0 0.9 %convert_reduce_fusion = f32[8,80]{1,0:T(8,128)S(1)} fusion(bf16[8,80,64]{1,2,0:T(8,128)(2,1)} %param.11), kind=kLoop, calls=%fused_computation.10 | loop fusion | flops 81280 | bytes 84480 | tf_op jit(solution)/shard_map/reduce_sum | solution.py:20
  2.9 1.0 %fusion.5 = f32[8,80]{1,0:T(8,128)S(1)} fusion(bf16[8,80,64]{1,2,0:T(8,128)(2,1)} %param.11, f32[8,80]{1,0:T(8,128)S(1)} %broadcast_multiply_fusion.3), kind=kLoop, calls=%fused_computation.13 | loop fusion | flops 163200 | bytes 87040 | tf_op jit(solution)/shard_map/reduce_sum | solution.py:21
  3.9 0.9 %fusion.6 = bf16[8,80,64]{1,2,0:T(8,128)(2,1)S(1)} fusion(bf16[8,80,64]{1,2,0:T(8,128)(2,1)} %param.11, f32[8,80]{1,0:T(8,128)S(1)} %add_rsqrt_fusion, f32[8,80]{1,0:T(8,128)S(1)} %broadcast_multiply_fusion.3), kind=kLoop, calls=%fused_computation.14 | loop fusion | flops 163840 | bytes 168960 | tf_op jit(solution)/shard_map/convert_element_type | solution.py:380
  4.9 0.1 broadcast_multiply_fusion.2
  5.0 0.8 %copy.32 = bf16[1,64,64]{1,2,0:T(8,128)(2,1)S(1)} copy(bf16[1,64,64]{2,1,0:T(8,128)(2,1)} %param.15) | data formatting | bytes 16384 | tf_op args[4]
  5.8 0.2 fusion.2
  5.9 0.8 %reshape.139.right_ref = bf16[8,2560]{1,0:T(8,128)(2,1)} reshape(bf16[8,32,80]{2,1,0:T(8,128)(2,1)S(1)} %fusion.2) | data formatting | bytes 81920 | tf_op jit(solution)/shard_map/reshape | solution.py:386
  6.7 0.1 fusion.1
  6.8 0.1 copy.33
  7.0 0.2 reshape.140
  7.2 0.6 copy.48
  7.8 0.7 %copy.45.normed_ref = bf16[80,512]{1,0:T(8,128)(2,1)} copy(bf16[80,512]{0,1:T(8,128)(2,1)S(1)} %bitcast.45) | data formatting | bytes 163840 | tf_op jit(solution)/shard_map/reshape | solution.py:381
  8.5 1.6 %copy.46.homolog_ref = bf16[80,512]{1,0:T(8,128)(2,1)} copy(bf16[80,512]{0,1:T(8,128)(2,1)} %bitcast.44) | data formatting | bytes 163840 | tf_op jit(solution)/shard_map/reshape | solution.py:436
  10.2 0.0 copy-done
  10.2 0.1 copy.37
  10.3 0.8 %copy.43.outer_w_ref = bf16[128,1024]{1,0:T(8,128)(2,1)} copy(bf16[128,1024]{0,1:T(8,128)(2,1)S(1)} %bitcast.46) | data formatting | bytes 524288 | tf_op jit(solution)/shard_map/reshape | solution.py:391
  11.1 0.0 copy-done.1
  11.1 0.1 copy.38
  11.2 1.0 %mul.115 = bf16[4,64,2,8,4,32]{1,0,5,4,3,2:T(4,128)(2,1)S(1)} broadcast(bf16[64,2,8,32]{0,3,2,1:T(8,128)(2,1)S(1)} %bitcast.48), dimensions={1,2,3,5} | broadcast | bytes 1114112 | tf_op jit(solution)/shard_map/mul | solution.py:394
  12.2 1.4 %mul.116 = bf16[256,2,1024]{0,2,1:T(8,128)(2,1)S(1)} reshape(bf16[4,64,2,8,4,32]{1,0,5,4,3,2:T(4,128)(2,1)S(1)} %mul.115) | data formatting | bytes 2097152 | tf_op jit(solution)/shard_map/mul | solution.py:394
  13.6 0.5 copy.40
  14.2 0.5 mul.117
  14.7 0.7 mul.118
  15.3 0.2 copy.39
  15.5 0.0 copy-start.2
  15.5 0.1 broadcast_multiply_fusion.1
  15.7 1.0 %slice_bitcast_fusion = (bf16[256,1024]{1,0:T(8,128)(2,1)}, bf16[256,1024]{1,0:T(8,128)(2,1)}) fusion(bf16[256,2,1024]{2,0,1:T(8,128)(2,1)S(1)} %broadcast_multiply_fusion.1), kind=kLoop, calls=%fused_computation.5 | loop fusion | bytes 2097152 | tf_op jit(solution)/shard_map/squeeze | solution.py:437
  16.7 0.1 copy.42
  16.8 0.0 copy-done.2
  16.8 0.1 copy.41
  16.9 0.5 broadcast_multiply_fusion
  17.4 1.5 %mul.125.final_w_ref = bf16[1024,256]{1,0:T(8,128)(2,1)} reshape(bf16[8,4,32,4,64]{4,3,2,1,0:T(4,128)(2,1)S(1)} %broadcast_multiply_fusion) | data formatting | bytes 1048576 | tf_op jit(solution)/shard_map/mul | solution.py:397
  18.9 49.0 %msa_block.1 = (bf16[80,512]{1,0:T(8,128)(2,1)}, bf16[40,80,128]{2,1,0:T(8,128)(2,1)}) custom-call(s32[1]{0:T(128)} %copy.50.seqs_ref, s32[1]{0:T(128)} %copy.51.length_ref, bf16[8,2560]{1,0:T(8,128)(2,1)} %reshape.139.right_ref, bf16[2,8,1280]{2,1,0:T(8,128)(2,1)} %bitcast.52, bf16[80,512]{1,0:T(8,128)(2,1)} %copy.45.normed_ref, ...), custom_call_target="tpu_custom_call" | custom-call | tf_op jit(solution)/shard_map/msa_block/pallas_call | solution.py:402
  67.9 1.0 %reshape.144 = bf16[80,8,64]{2,1,0:T(8,128)(2,1)S(1)} reshape(bf16[80,512]{1,0:T(8,128)(2,1)} %get-tuple-element.4) | data formatting | bytes 163840 | tf_op jit(solution)/shard_map/reshape | solution.py:440
  69.0 0.8 %copy.44 = bf16[8,80,64]{1,2,0:T(8,128)(2,1)} copy(bf16[8,80,64]{2,0,1:T(8,128)(2,1)S(1)} %bitcast.47) | data formatting | bytes 163840
  69.8 2.1 %copy.52 = bf16[40,80,128]{2,1,0:T(8,128)(2,1)} copy(bf16[40,80,128]{2,1,0:T(8,128)(2,1)} %get-tuple-element.15) | data formatting | bytes 1638400
  (5 shorter events, 0.0 us)
Async XLA Ops:
  0.6 9.5 %copy-start = (bf16[1,1024,128]{2,1,0:T(8,128)(2,1)S(1)}, bf16[1,1024,128]{2,1,0:T(8,128)(2,1)}, u32[]{:S(2)}) copy-start(bf16[1,1024,128]{2,1,0:T(8,128)(2,1)} %param.16) | copy-start | bytes 786436
  0.6 10.5 %copy-start.1 = (bf16[1,64,512]{2,1,0:T(8,128)(2,1)S(1)}, bf16[1,64,512]{2,1,0:T(8,128)(2,1)}, u32[]{:S(2)}) copy-start(bf16[1,64,512]{2,1,0:T(8,128)(2,1)} %param.17) | copy-start | bytes 196612
  15.5 1.3 %copy-start.2 = (bf16[1,256,64]{1,2,0:T(8,128)(2,1)S(1)}, bf16[1,256,64]{1,2,0:T(8,128)(2,1)}, u32[]{:S(2)}) copy-start(bf16[1,256,64]{1,2,0:T(8,128)(2,1)} %param.19) | copy-start | bytes 98308

commit v4 on v3

--- a/solution.py
+++ b/solution.py
@@ -35,10 +35,11 @@
     dims,
     seqs_ref, length_ref,
     right_ref, left_ref, normed_ref, homolog_ref, pair_ref,
-    outer_w_ref, value_w_ref, gate_w_ref, logit_w_ref, final_w_ref, up_ref, down_ref,
+    outer_w_ref, mix_ref, logit_w_ref, mix_out_ref, up_ref, down_ref,
     msa_ref, out_ref,
     right_buf, left_buf, normed_buf, logit_send, logit_buf, stat_send, stat_buf, expo_tile,
     right_all, left_all, product, pair_new, pair_normed, values, gates, gated,
+    value_w_ref, gate_w_ref, final_w_ref,
     s_right, r_right, s_left, r_left, s_norm, r_norm, s_logit, r_logit, s_stat, r_stat,
 ):
     R, C, ratio, rows, cols, width, heads, chunks = dims
@@ -140,6 +141,28 @@
             src_ref=normed_ref, dst_ref=normed_buf.at[src],
             send_sem=s_norm.at[0], recv_sem=r_norm.at[src],
             device_id=(r, src), device_id_type=MESH).wait_recv()
+
+    feats, hidden_width = mix_out_ref.shape
+    head_width = hidden_width // heads
+    pack = LANES // head_width
+    shape = (pack * feats, feats)
+    stack = (lax.broadcasted_iota(jnp.int32, shape, 0) % feats
+             == lax.broadcasted_iota(jnp.int32, shape, 1)).astype(F32).astype(BF16)
+    shape = (hidden_width, heads * LANES)
+    row, lane = (lax.broadcasted_iota(jnp.int32, shape, axis) for axis in (0, 1))
+    widen = ((row // head_width == lane // LANES) & (row % head_width == lane % head_width))
+    widen = widen.astype(F32).astype(BF16)
+    shape = (pack * feats, heads * LANES)
+    row, lane = (lax.broadcasted_iota(jnp.int32, shape, axis) for axis in (0, 1))
+    diagonal = row // feats == lane % LANES // head_width
+    for source, target in (
+        (mix_ref[:, :hidden_width], value_w_ref),
+        (mix_ref[:, hidden_width:], gate_w_ref),
+        (mix_out_ref[...], final_w_ref),
+    ):
+        tall = jnp.dot(stack, source, preferred_element_type=F32).astype(BF16)
+        wide = jnp.dot(tall, widen, preferred_element_type=F32)
+        target[...] = jnp.where(diagonal, wide, 0.0).astype(BF16)
 
     for n in sorted(range(1, R), key=lambda n: (bin(n).count("1"), -(n & -n))):
         wait_right(n)
@@ -309,11 +332,12 @@
             at = (g * heads + h) * LANES
             gated[:, at:at + LANES] = mixed[:, g * LANES:(g + 1) * LANES]
     for g in range(groups):
-        part = jnp.dot(
+        part = lax.dot_general(
             gated[:, g * heads * LANES:(g + 1) * heads * LANES], final_w_ref[...],
-            preferred_element_type=F32)
-        sl = slice(g * group_width, (g + 1) * group_width)
-        msa_ref[:, sl] = (homolog_ref[:, sl].astype(F32) + part).astype(BF16)
+            (((1,), (1,)), ((), ())), preferred_element_type=F32)
+        sl = slice(g * pack, (g + 1) * pack)
+        msa_ref[sl] = (
+            homolog_ref[sl].astype(F32) + part.T.reshape(pack, feats, cols)).astype(BF16)
 
     for t in range(1, R):
         right_copy(t).wait_send()
@@ -376,7 +400,7 @@
     res_ids = c * cols + jnp.arange(cols, dtype=jnp.int32)
     seq_float = (seq_ids < genuine_homolog_total[0]).astype(F32)
     res_float = (res_ids < genuine_chain_length[0]).astype(F32)
-    flipped = homolog_matrix.transpose(1, 0, 2)
+    flipped = homolog_matrix.transpose(0, 2, 1)
     normed = standardize_features(homolog_matrix).astype(BF16)
     normed_flat = normed.transpose(1, 0, 2).reshape(cols, seqs * feats)
     left_w = tensor_product_matrices[0][:, :ch]
@@ -389,12 +413,6 @@
     left = left.reshape(seqs, ratio, rows * ch).transpose(1, 0, 2)
     outer_w = tensor_product_final[0].reshape(ch, ch, pair_width).transpose(2, 1, 0)
     outer_w = outer_w.reshape(pair_width, ch * ch)
-    same = jnp.eye(pack, dtype=BF16)
-    vg = mixing_value_gate_matrix[0].reshape(feats, 2, heads, head_width)
-    spread = vg[None, :, :, :, None, :] * same[:, None, None, None, :, None]
-    spread = spread.reshape(pack * feats, 2, heads * LANES)
-    final = mixing_final_matrix[0].reshape(heads, 1, head_width, 1, feats)
-    final = (final * same[None, :, None, :, None]).reshape(heads * LANES, pack * feats)
     dims = (R, C, ratio, rows, cols, seqs * feats, heads, chunks)
     vmem = pl.BlockSpec(memory_space=pltpu.VMEM)
     smem = pl.BlockSpec(memory_space=pltpu.SMEM)
@@ -402,10 +420,10 @@
     msa, pair_out = pl.pallas_call(
         functools.partial(kernel, dims),
         out_shape=(
-            jax.ShapeDtypeStruct((cols, seqs * feats), BF16),
+            jax.ShapeDtypeStruct(flipped.shape, BF16),
             jax.ShapeDtypeStruct(contact_matrix.shape, BF16),
         ),
-        in_specs=[smem] * 2 + [vmem] * 12,
+        in_specs=[smem] * 2 + [vmem] * 11,
         out_specs=(vmem, vmem),
         scratch_shapes=[
             pltpu.VMEM((R, seqs, ch * cols), BF16),
@@ -424,6 +442,9 @@
             pltpu.VMEM((C * LANES, heads * groups * LANES), BF16),
             pltpu.VMEM((cols, heads * groups * LANES), F32),
             pltpu.VMEM((cols, heads * groups * LANES), BF16),
+            pltpu.VMEM((pack * feats, heads * LANES), BF16),
+            pltpu.VMEM((pack * feats, heads * LANES), BF16),
+            pltpu.VMEM((pack * feats, heads * LANES), BF16),
             dma((R,)), dma((R,)), dma((ratio, C)), dma((R,)), dma((C,)), dma((C,)),
             dma((chunks, R)), dma((ratio, C, chunks)), dma((R,)), dma((ratio, C)),
         ],
@@ -433,11 +454,11 @@
         name="msa_block",
     )(
         genuine_homolog_total, genuine_chain_length,
-        right, left, normed_flat, flipped.reshape(cols, seqs * feats), contact_matrix,
-        outer_w, spread[:, 0], spread[:, 1], mixing_logit_matrix[0].T, final,
+        right, left, normed_flat, flipped, contact_matrix,
+        outer_w, mixing_value_gate_matrix[0], mixing_logit_matrix[0].T, mixing_final_matrix[0].T,
         feedforward_gate_expand[0], feedforward_shrink_matrix[0],
     )
-    return (msa.reshape(cols, seqs, feats).transpose(1, 0, 2), pair_out)
+    return (msa.transpose(0, 2, 1), pair_out)
 
 
 def solution(mesh):

time: 72.3 us -> 60.4 us (0.84)
  local copies, waits for them, and re-layouts: 16.9 us -> 7.79 us
  other arithmetic: 3.52 us -> 1.14 us
    mul x7 -> x0, local copies, waits for them, and re-layouts: 5.73 us -> none  [the longest x6 4.24 us: local(): spread = vg[None, :, :, :, None, :] * same[:, None, None, None, :, None]]
    reshape x2 -> x0, local copies, waits for them, and re-layouts: 2.68 us -> none  [the longest x1 1.64 us: local(): flipped.reshape(cols, seqs * feats)]
    squeeze x1 -> x0, local copies, waits for them, and re-layouts: 1.05 us -> none  [local(): spread[:, 1]]
    reduce_sum x1, other arithmetic: 0.96 us -> 0.06 us  [standardize_features(): spread = jnp.mean(center * center, axis=-1, keepdims=True)]
    convert_element_type x1, other arithmetic: 0.95 us -> 0.05 us  [local(): normed = standardize_features(homolog_matrix).astype(BF16)]
    unnamed x11 -> x9, local copies, waits for them, and re-layouts: 3.94 us -> 4.39 us
where the time goes in v4:
time: 60.4 us; the launch traced here: 60.1 us
  Pallas kernels  48.8 us (81%)
  local copies, waits for them, and re-layouts  7.79 us (13%)
  between operations  2.06 us (3%)
  other arithmetic  1.14 us (2%)
    pallas_call x1, Pallas kernels, local(): pl.pallas_call(functools.partial(kernel, dims), out_shape=(jax.ShapeDtype...  48.8 us
    unnamed x9, local copies, waits for them, and re-layouts  4.39 us

profile of v4, /device:TPU:0, one launch (start us, length us, event | category | flops | bytes accessed | tf_op | source)
XLA Modules:
  0.0 60.1 jit_solution(8202271495704563819)
XLA Ops:
  0.6 0.0 copy-start
  2.0 0.1 broadcast_multiply_fusion
  2.1 0.9 %convert_reduce_fusion = f32[8,80]{1,0:T(8,128)S(1)} fusion(bf16[8,80,64]{1,2,0:T(8,128)(2,1)} %param.11), kind=kLoop, calls=%fused_computation.6 | loop fusion | flops 81280 | bytes 84480 | tf_op jit(solution)/shard_map/reduce_sum | solution.py:20
  3.0 0.0 copy-done
  3.0 0.0 copy-start.2
  3.0 0.1 fusion.5
  3.1 0.6 %copy-done.2 = bf16[1,64,64]{2,1,0:T(8,128)(2,1)S(1)} copy-done((bf16[1,64,64]{2,1,0:T(8,128)(2,1)S(1)}, bf16[1,64,64]{2,1,0:T(8,128)(2,1)}, u32[]{:S(2)}) %copy-start.2) | copy-done | bytes 8216
  3.8 0.1 copy.21
  3.9 0.1 fusion.2
  4.1 0.8 %reshape.108.right_ref = bf16[8,2560]{1,0:T(8,128)(2,1)} reshape(bf16[8,32,80]{2,1,0:T(8,128)(2,1)S(1)} %fusion.2) | data formatting | bytes 81920 | tf_op jit(solution)/shard_map/reshape | solution.py:410
  4.8 0.1 fusion.1
  5.0 0.7 %copy.27.normed_ref = bf16[80,512]{1,0:T(8,128)(2,1)} copy(bf16[80,512]{0,1:T(8,128)(2,1)S(1)} %bitcast.37) | data formatting | bytes 163840 | tf_op jit(solution)/shard_map/reshape | solution.py:405
  5.7 0.0 copy-start.1
  5.7 0.1 copy.22
  5.8 0.2 reshape.109
  6.0 0.6 %copy.29 = bf16[8,2,1280]{2,0,1:T(8,128)(2,1)} copy(bf16[8,2,1280]{2,1,0:T(2,128)(2,1)S(1)} %reshape.109) | data formatting | bytes 81920 | tf_op jit(solution)/shard_map/reshape | solution.py:413
  6.7 0.0 copy-done.1
  6.7 0.1 copy.25
  6.8 0.9 %copy.26.outer_w_ref = bf16[128,1024]{1,0:T(8,128)(2,1)} copy(bf16[128,1024]{0,1:T(8,128)(2,1)S(1)} %bitcast.38) | data formatting | bytes 524288 | tf_op jit(solution)/shard_map/reshape | solution.py:415
  7.6 48.8 %msa_block.1 = (bf16[8,64,80]{2,1,0:T(8,128)(2,1)}, bf16[40,80,128]{2,1,0:T(8,128)(2,1)}) custom-call(s32[1]{0:T(128)} %copy.32.seqs_ref, s32[1]{0:T(128)} %copy.33.length_ref, bf16[8,2560]{1,0:T(8,128)(2,1)} %reshape.108.right_ref, bf16[2,8,1280]{2,1,0:T(8,128)(2,1)} %bitcast.41, bf16[80,512]{1,0:T(8,128)(2,1)} %copy.27.normed_ref, ...), custom_call_target="tpu_custom_call" | custom-call | tf_op jit(solution)/shard_map/msa_block/pallas_call | solution.py:420
  56.4 1.6 %copy.34 = bf16[8,80,64]{1,2,0:T(8,128)(2,1)} copy(bf16[8,80,64]{1,2,0:T(8,128)(2,1)} %bitcast.43) | data formatting | bytes 163840
  58.0 2.1 %copy.35 = bf16[40,80,128]{2,1,0:T(8,128)(2,1)} copy(bf16[40,80,128]{2,1,0:T(8,128)(2,1)} %get-tuple-element.9) | data formatting | bytes 1638400
  (5 shorter events, 0.1 us)
Async XLA Ops:
  0.6 2.4 %copy-start = (bf16[8,80,64]{1,2,0:T(8,128)(2,1)S(1)}, bf16[8,80,64]{1,2,0:T(8,128)(2,1)}, u32[]{:S(2)}) copy-start(bf16[8,80,64]{1,2,0:T(8,128)(2,1)} %param.11) | copy-start | bytes 245764
  3.0 0.7 %copy-start.2 = (bf16[1,64,64]{2,1,0:T(8,128)(2,1)S(1)}, bf16[1,64,64]{2,1,0:T(8,128)(2,1)}, u32[]{:S(2)}) copy-start(bf16[1,64,64]{2,1,0:T(8,128)(2,1)} %param.15) | copy-start | bytes 24580
  5.7 1.0 %copy-start.1 = (bf16[1,1024,128]{2,1,0:T(8,128)(2,1)S(1)}, bf16[1,1024,128]{2,1,0:T(8,128)(2,1)}, u32[]{:S(2)}) copy-start(bf16[1,1024,128]{2,1,0:T(8,128)(2,1)} %param.16) | copy-start | bytes 786436

commit v5 on v4

--- a/solution.py
+++ b/solution.py
@@ -34,12 +34,12 @@
 def kernel(
     dims,
     seqs_ref, length_ref,
-    right_ref, left_ref, normed_ref, homolog_ref, pair_ref,
-    outer_w_ref, mix_ref, logit_w_ref, mix_out_ref, up_ref, down_ref,
+    homolog_ref, pair_ref, project_ref,
+    outer_ref, mix_ref, logit_w_ref, mix_out_ref, up_ref, down_ref,
     msa_ref, out_ref,
     right_buf, left_buf, normed_buf, logit_send, logit_buf, stat_send, stat_buf, expo_tile,
     right_all, left_all, product, pair_new, pair_normed, values, gates, gated,
-    value_w_ref, gate_w_ref, final_w_ref,
+    value_w_ref, gate_w_ref, final_w_ref, right_ref, left_ref, normed_ref, tile_a, tile_b, outer_w_ref, outer_f32,
     s_right, r_right, s_left, r_left, s_norm, r_norm, s_logit, r_logit, s_stat, r_stat,
 ):
     R, C, ratio, rows, cols, width, heads, chunks = dims
@@ -70,6 +70,33 @@
             @pl.when(jnp.logical_not((row == r) & (col == c)))
             def _():
                 greet(row, col)
+
+    seqs, feats, _ = homolog_ref.shape
+    half_width = project_ref.shape[1] // 2
+    field = homolog_ref[...].astype(F32)
+    center = field - jnp.mean(field, axis=1, keepdims=True)
+    spread = jnp.mean(center * center, axis=1, keepdims=True)
+    normed_t = center * lax.rsqrt(spread + EPSILON)
+    normed_ref[...] = normed_t.reshape(width, cols).T.astype(BF16)
+    project_t = project_ref[...].astype(F32).T.astype(BF16)
+    along = c * cols + lax.broadcasted_iota(jnp.int32, (half_width, cols), 1) < length_ref[0]
+    down = c * cols + lax.broadcasted_iota(jnp.int32, (cols, half_width), 0) < length_ref[0]
+    for n in range(seqs):
+        there = r * seqs + n < seqs_ref[0]
+        side = jnp.dot(
+            project_t[half_width:], normed_t[n].astype(BF16), preferred_element_type=F32)
+        tile_a[n * half_width:(n + 1) * half_width, 0:cols] = jnp.where(along & there, side, 0.0)
+        side = jnp.dot(
+            normed_ref[:, n * feats:(n + 1) * feats], project_ref[:, :half_width],
+            preferred_element_type=F32)
+        tile_b[n * cols:(n + 1) * cols, 0:half_width] = jnp.where(down & there, side, 0.0)
+    right_ref[...] = jnp.concatenate(
+        [tile_a[pl.ds(d, seqs, stride=half_width), :][:, :cols] for d in range(half_width)],
+        axis=1).astype(BF16)
+    for h in range(ratio):
+        left_ref[h] = jnp.concatenate(
+            [tile_b[pl.ds(h * rows + i, seqs, stride=cols), :][:, :half_width]
+             for i in range(rows)], axis=1).astype(BF16)
 
     own = jnp.where(home == c, 1, 0)
     pl.semaphore_wait(barrier, (R - 1) + (C - 1) + 2 * R - 2 * own)
@@ -142,7 +169,14 @@
             send_sem=s_norm.at[0], recv_sem=r_norm.at[src],
             device_id=(r, src), device_id_type=MESH).wait_recv()
 
-    feats, hidden_width = mix_out_ref.shape
+    outer_f32[...] = outer_ref[...].astype(F32)
+    quad = LANES // half_width
+    for d in range(0, half_width, quad):
+        outer_w_ref[:, d * half_width:(d + quad) * half_width] = jnp.concatenate(
+            [outer_f32[pl.ds(d + e, half_width, stride=half_width), :] for e in range(quad)],
+            axis=0).T.astype(BF16)
+
+    hidden_width = mix_out_ref.shape[1]
     head_width = hidden_width // heads
     pack = LANES // head_width
     shape = (pack * feats, feats)
@@ -394,25 +428,7 @@
     chunks = rows // 8
     pack = LANES // head_width
     groups = seqs // pack
-    r = lax.axis_index("row")
-    c = lax.axis_index("col")
-    seq_ids = r * seqs + jnp.arange(seqs, dtype=jnp.int32)
-    res_ids = c * cols + jnp.arange(cols, dtype=jnp.int32)
-    seq_float = (seq_ids < genuine_homolog_total[0]).astype(F32)
-    res_float = (res_ids < genuine_chain_length[0]).astype(F32)
     flipped = homolog_matrix.transpose(0, 2, 1)
-    normed = standardize_features(homolog_matrix).astype(BF16)
-    normed_flat = normed.transpose(1, 0, 2).reshape(cols, seqs * feats)
-    left_w = tensor_product_matrices[0][:, :ch]
-    right_w = tensor_product_matrices[0][:, ch:]
-    right = jnp.einsum("sjf,fd->sdj", normed, right_w, preferred_element_type=F32)
-    right = (right * (seq_float[:, None, None] * res_float[None, None, :])).astype(BF16)
-    right = right.reshape(seqs, ch * cols)
-    left = jnp.einsum("sjf,fc->sjc", normed, left_w, preferred_element_type=F32)
-    left = (left * (seq_float[:, None, None] * res_float[None, :, None])).astype(BF16)
-    left = left.reshape(seqs, ratio, rows * ch).transpose(1, 0, 2)
-    outer_w = tensor_product_final[0].reshape(ch, ch, pair_width).transpose(2, 1, 0)
-    outer_w = outer_w.reshape(pair_width, ch * ch)
     dims = (R, C, ratio, rows, cols, seqs * feats, heads, chunks)
     vmem = pl.BlockSpec(memory_space=pltpu.VMEM)
     smem = pl.BlockSpec(memory_space=pltpu.SMEM)
@@ -423,7 +439,7 @@
             jax.ShapeDtypeStruct(flipped.shape, BF16),
             jax.ShapeDtypeStruct(contact_matrix.shape, BF16),
         ),
-        in_specs=[smem] * 2 + [vmem] * 11,
+        in_specs=[smem] * 2 + [vmem] * 9,
         out_specs=(vmem, vmem),
         scratch_shapes=[
             pltpu.VMEM((R, seqs, ch * cols), BF16),
@@ -445,6 +461,13 @@
             pltpu.VMEM((pack * feats, heads * LANES), BF16),
             pltpu.VMEM((pack * feats, heads * LANES), BF16),
             pltpu.VMEM((pack * feats, heads * LANES), BF16),
+            pltpu.VMEM((seqs, ch * cols), BF16),
+            pltpu.VMEM((ratio, seqs, rows * ch), BF16),
+            pltpu.VMEM((cols, seqs * feats), BF16),
+            pltpu.VMEM((seqs * ch, LANES), F32),
+            pltpu.VMEM((seqs * cols, LANES), F32),
+            pltpu.VMEM((pair_width, ch * ch), BF16),
+            pltpu.VMEM((ch * ch, pair_width), F32),
             dma((R,)), dma((R,)), dma((ratio, C)), dma((R,)), dma((C,)), dma((C,)),
             dma((chunks, R)), dma((ratio, C, chunks)), dma((R,)), dma((ratio, C)),
         ],
@@ -454,8 +477,8 @@
         name="msa_block",
     )(
         genuine_homolog_total, genuine_chain_length,
-        right, left, normed_flat, flipped, contact_matrix,
-        outer_w, mixing_value_gate_matrix[0], mixing_logit_matrix[0].T, mixing_final_matrix[0].T,
+        flipped, contact_matrix, tensor_product_matrices[0],
+        tensor_product_final[0], mixing_value_gate_matrix[0], mixing_logit_matrix[0].T, mixing_final_matrix[0].T,
         feedforward_gate_expand[0], feedforward_shrink_matrix[0],
     )
     return (msa.transpose(0, 2, 1), pair_out)

time: 60.4 us -> 54.6 us (0.904)
  local copies, waits for them, and re-layouts: 7.79 us -> 3.66 us
  other arithmetic: 1.14 us -> 0 us
    reshape x5 -> x0, local copies, waits for them, and re-layouts: 3.16 us -> none  [the longest x1 0.85 us: local(): outer_w = outer_w.reshape(pair_width, ch * ch)]
    reduce_sum x2 -> x0, other arithmetic: 1 us -> none  [the longest x1 0.94 us: standardize_features(): center = field - jnp.mean(field, axis=-1, keepdims=True)]
    unnamed x9 -> x2, local copies, waits for them, and re-layouts: 4.39 us -> 3.66 us
where the time goes in v5:
time: 54.6 us; the launch traced here: 54.4 us
  Pallas kernels  48.8 us (89%)
  local copies, waits for them, and re-layouts  3.66 us (7%)
  between operations  1.93 us (4%)
    pallas_call x1, Pallas kernels, local(): pl.pallas_call(functools.partial(kernel, dims), out_shape=(jax.ShapeDtype...  48.8 us
    unnamed x2, local copies, waits for them, and re-layouts  3.66 us

profile of v5, /device:TPU:0, one launch (start us, length us, event | category | flops | bytes accessed | tf_op | source)
XLA Modules:
  0.0 54.4 jit_solution(14883545515465777492)
XLA Ops:
  1.9 48.8 %msa_block.1 = (bf16[8,64,80]{2,1,0:T(8,128)(2,1)}, bf16[40,80,128]{2,1,0:T(8,128)(2,1)}) custom-call(s32[1]{0:T(128)S(6)} %copy.15.seqs_ref, s32[1]{0:T(128)S(6)} %copy.16.length_ref, bf16[8,64,80]{2,1,0:T(8,128)(2,1)} %bitcast.15, bf16[40,80,128]{2,1,0:T(8,128)(2,1)} %pair_ref.1, bf16[64,64]{1,0:T(8,128)(2,1)} %bitcast.20, bf16[1024,128]{1,0:T(8,128)(2,1)} %bitcast.13, ...), custom_call_target="tpu_custom_call" | custom-call | tf_op jit(solution)/shard_map/msa_block/pallas_call | solution.py:436
  50.7 1.6 %copy.17 = bf16[8,80,64]{1,2,0:T(8,128)(2,1)} copy(bf16[8,80,64]{1,2,0:T(8,128)(2,1)} %bitcast.17) | data formatting | bytes 163840
  52.3 2.1 %copy.18 = bf16[40,80,128]{2,1,0:T(8,128)(2,1)} copy(bf16[40,80,128]{2,1,0:T(8,128)(2,1)} %get-tuple-element.9) | data formatting | bytes 1638400

commit v6 on v5

--- a/solution.py
+++ b/solution.py
@@ -133,6 +133,9 @@
             send_sem=s_stat.at[t], recv_sem=r_stat.at[r % ratio, c],
             device_id=((r + t) % R, home), device_id_type=MESH)
 
+    steps = [R >> (e + 1) for e in range(R.bit_length() - 1)]
+    for bit in steps:
+        right_copy(bit).start()
     for h in range(ratio):
         for t in range(C):
             mine = (c * ratio + h == r) & (t == 0)
@@ -145,9 +148,6 @@
             def _():
                 left_buf[r] = left_ref[h]
 
-    steps = [R >> (e + 1) for e in range(R.bit_length() - 1)]
-    for bit in steps:
-        right_copy(bit).start()
     right_buf[r] = right_ref[...]
     normed_buf[c] = normed_ref[...]
 

time: 54.6 us -> 50.3 us (0.921)
  Pallas kernels: 48.8 us -> 44.4 us
    pallas_call x1, Pallas kernels: 48.8 us -> 44.4 us  [local(): pl.pallas_call(functools.partial(kernel, dims), out_shape=(jax.ShapeDtype...]
where the time goes in v6:
time: 50.3 us; the launch traced here: 50 us
  Pallas kernels  44.4 us (88%)
  local copies, waits for them, and re-layouts  3.66 us (7%)
  between operations  1.93 us (4%)
    pallas_call x1, Pallas kernels, local(): pl.pallas_call(functools.partial(kernel, dims), out_shape=(jax.ShapeDtype...  44.4 us
    unnamed x2, local copies, waits for them, and re-layouts  3.66 us

profile of v6, /device:TPU:0, one launch (start us, length us, event | category | flops | bytes accessed | tf_op | source)
XLA Modules:
  0.0 50.0 jit_solution(6392680816284937693)
XLA Ops:
  1.9 44.4 %msa_block.1 = (bf16[8,64,80]{2,1,0:T(8,128)(2,1)}, bf16[40,80,128]{2,1,0:T(8,128)(2,1)}) custom-call(s32[1]{0:T(128)S(6)} %copy.15.seqs_ref, s32[1]{0:T(128)S(6)} %copy.16.length_ref, bf16[8,64,80]{2,1,0:T(8,128)(2,1)} %bitcast.15, bf16[40,80,128]{2,1,0:T(8,128)(2,1)} %pair_ref.1, bf16[64,64]{1,0:T(8,128)(2,1)} %bitcast.20, bf16[1024,128]{1,0:T(8,128)(2,1)} %bitcast.13, ...), custom_call_target="tpu_custom_call" | custom-call | tf_op jit(solution)/shard_map/msa_block/pallas_call | solution.py:436
  46.3 1.6 %copy.17 = bf16[8,80,64]{1,2,0:T(8,128)(2,1)} copy(bf16[8,80,64]{1,2,0:T(8,128)(2,1)} %bitcast.17) | data formatting | bytes 163840
  47.9 2.1 %copy.18 = bf16[40,80,128]{2,1,0:T(8,128)(2,1)} copy(bf16[40,80,128]{2,1,0:T(8,128)(2,1)} %get-tuple-element.9) | data formatting | bytes 1638400
